TPU v7x, 32 devices: a whole 2x2x4 slice. The times are simulated.
32 devices in a mesh: site: 8 (over z, x), real: 4 (over y, core).
Axes of the slice: x: 2, y: 2, z: 4, core: 2. Of those that a mesh axis runs over, the one named last changes fastest.
Arguments:
- epsilon: bfloat16 [8192, 2048], P('site', 'real'), may hold values from -6 to 6
- factor: bfloat16 [2, 72, 512, 512], P(None, 'site'), may hold values from -0.09375 to 0.09375
- block_rows: int32 [2, 72], P(None, 'site'), may hold values from 0 to 15, as said below
- median_log: float32 [8192], P('site'), may hold values from -2.5 to -0.5
- spread_log: float32 [8192], P('site'), may hold values from 0.4 to 0.8
- critical_yield: float32 [8192], P('site'), may hold values from 0.03 to 0.3
Outputs:
- residual_field: bfloat16 [8192, 2048], P('site', 'real')
- mean_damage: float32 [8192], P('site')
Inputs may be any that keep to these rules, and one draw needn't show every extreme that they name: block_rows[p, b] = (c + o) mod 16, with c = 2 * (b // 9) + p the block's column tile and o in 0 to 11; the offsets o of one block column are distinct, and the first block of each column has o = 0.
All inputs are finite; a program needn't handle non-finite values.
Results may differ from a plain program's by a relative error of at most 0.001.
Values sent between devices are 32-bit elements; how exact they have to be, the bound alone decides.
A program may use at most 256 MiB of HBM per device.

v0:
```python
import functools
import jax
import jax.numpy as jnp
from jax import lax
from jax.experimental import pallas as pl
from jax.experimental.pallas import tpu as pltpu
from jax.sharding import PartitionSpec as P

BAND = 12
PAIR = 2
LANES = 128
ROWS = 64
AHEAD = 6
PARTS = 4
HEAD = 2
LAG = 1
MESH = pl.DeviceIdType.MESH

coeff_disp = 10.0**0.215
power_margin = 2.341
power_ratio = 1.438


def passed_along(value, axis, steps):
    count = lax.axis_size(axis)
    pairs = [(source, (source + steps) % count) for source in range(count)]
    return lax.ppermute(value, axis, pairs)


def shards(epsilon, factor, block_rows, median_log, spread_log, critical_yield):
    panels = factor.shape[0]
    per_column = factor.shape[1]
    tile_size = factor.shape[-1]
    own_reals = epsilon.shape[1]
    reach = BAND // 2
    own_index = lax.axis_index("site")
    total_tiles = panels * lax.axis_size("site")
    draws = epsilon.reshape(panels, tile_size, own_reals)

    def pending(panel):
        flat = factor[panel].reshape(per_column * tile_size, tile_size)
        products = jnp.dot(flat, draws[panel], preferred_element_type=jnp.float32)
        products = products.reshape(per_column, tile_size, own_reals)
        relative = (block_rows[panel] - own_index * panels) % total_tiles
        slots = jnp.zeros(((reach + 1) * panels, tile_size, own_reals), jnp.float32)
        sums = slots.at[relative].set(products, unique_indices=True)
        return sums.reshape(reach + 1, panels, tile_size, own_reals)

    combined = pending(0)
    panel = 1
    combined = combined + pending(panel)
    arrived = combined[0]
    for offset in range(1, reach + 1):
        arrived = arrived + passed_along(combined[offset], "site", offset)
    residual_field = arrived.astype(jnp.bfloat16).reshape(panels * tile_size, own_reals)
    log_peak = median_log[:, None] + spread_log[:, None] * residual_field.astype(jnp.float32)
    log_ratio = jnp.log(critical_yield)[:, None] - log_peak
    ratio = jnp.exp(log_ratio)
    margin = jnp.maximum(1.0 - ratio, 0.0)
    displacement = coeff_disp * jnp.power(margin, power_margin) * jnp.exp(-power_ratio * log_ratio)
    local_total = jnp.sum(jnp.log1p(displacement), axis=1)
    total = lax.psum(local_total, "real")
    mean_damage = total / (own_reals * lax.axis_size("real"))
    return (residual_field, mean_damage)


def field_kernel(
    depth, own_reals, block_rows, eps_in, factor_in, median, spread, critical, field_out, mean_out,
    eps, factor, head, x_out, x_in, z_out, z_in, totals, columns, folds, table, field,
    load_sem, x_send, x_recv, z_send, z_recv, t_send, t_recv, f_send,
):
    panels, per_column, tile = factor.shape[0], factor.shape[1], factor.shape[2]
    chunks = panels * tile // ROWS
    per_tile = tile // ROWS
    stages = depth - 1
    steps = stages * chunks
    reals = lax.axis_size("real")
    site = lax.axis_index("site")
    me = lax.axis_index("real")
    z, x = site // PAIR, site % PAIR

    first = [pltpu.make_async_copy(eps_in, eps, load_sem.at[0])]
    rest = []
    for panel in range(panels):
        first.append(pltpu.make_async_copy(
            factor_in.at[panel, :, :head.shape[2], :], head.at[panel], load_sem.at[1 + panel]
        ))
        rest.append(pltpu.make_async_copy(
            factor_in.at[panel], factor.at[panel], load_sem.at[1 + panels + panel]
        ))
    for load in first + rest:
        load.start()

    barrier = pltpu.get_barrier_semaphore()
    pl.semaphore_signal(barrier, inc=1, device_id={"site": site + 1 - 2 * x}, device_id_type=MESH)
    for shift in range(1, reals):
        pl.semaphore_signal(barrier, inc=1, device_id={"real": (me + shift) % reals}, device_id_type=MESH)

    @pl.when(z > 0)
    def _():
        pl.semaphore_signal(barrier, inc=1, device_id={"site": site - PAIR}, device_id_type=MESH)

    @pl.when(z < depth - 1)
    def _():
        pl.semaphore_signal(barrier, inc=1, device_id={"site": site + PAIR}, device_id_type=MESH)

    for panel in range(panels):
        begins = [
            (block_rows[panel, block] - site * panels + panels * PAIR * depth) % (panels * PAIR * depth)
            for block in range(per_column)
        ]

        @pl.loop(0, table.shape[1])
        def _(slot):
            number, found = jnp.int32(0), jnp.int32(0)
            for block in range(per_column):
                hit = begins[block] == slot
                number = jnp.where(hit, block, number)
                found = jnp.where(hit, 1, found)
            table[panel, slot] = number
            table[panels + panel, slot] = found

    pl.semaphore_wait(barrier, reals + jnp.where(z > 0, 1, 0) + jnp.where(z < depth - 1, 1, 0))

    for load in first:
        load.wait()

    def partial(offset, chunk, source=factor):
        relative = panels * offset + chunk // per_tile
        row = pl.multiple_of((chunk % per_tile) * ROWS, ROWS)
        result = None
        for panel in range(panels):
            block = source[panel, table[panel, relative], pl.ds(row, ROWS), :]
            product = jnp.dot(
                block, eps[panel * tile:(panel + 1) * tile, :], preferred_element_type=jnp.float32
            ) * table[panels + panel, relative].astype(jnp.float32)
            result = product if result is None else result + product
        return result

    low = 2 * z < depth

    def target(stage):
        falling = depth - 1 - stage
        of_low = jnp.where(falling > z, falling, stage - (depth - 1 - z))
        of_high = jnp.where(stage < z, stage, depth - 1 - (stage - z))
        of_stage = jnp.where(low, of_low, of_high)
        return jnp.where(stage == stages, z, of_stage)

    skipped = jnp.where(z == 0, 0, jnp.where(low, stages - 1, z - 1))

    def x_copy(group, chunk):
        return pltpu.make_async_remote_copy(
            src_ref=x_out.at[group, chunk],
            dst_ref=x_in.at[group, chunk],
            send_sem=x_send.at[group, chunk],
            recv_sem=x_recv.at[group, chunk],
            device_id={"site": site + 1 - 2 * x},
            device_id_type=MESH,
        )

    def group_of(turn):
        return jnp.where(x == 0, jnp.where(turn >= skipped, turn + 1, turn), turn)

    def x_step(step, source=factor):
        group, chunk = group_of(step // chunks), step % chunks
        offset = (PAIR * (target(group) - z + depth) + 1 - 2 * x) % (PAIR * depth)
        x_out[group, chunk] = partial(offset, chunk, source)
        x_copy(group, chunk).start()

    def z_copy(side, dest, chunk, stage, there):
        return pltpu.make_async_remote_copy(
            src_ref=z_out.at[stage, chunk],
            dst_ref=z_in.at[side, dest, chunk],
            send_sem=z_send.at[stage, chunk],
            recv_sem=z_recv.at[side, dest, chunk],
            device_id={"site": there},
            device_id_type=MESH,
        )

    def arrived(side, dest, chunk):
        z_copy(side, dest, chunk, 0, (site + PAIR) % (PAIR * depth)).wait_recv()
        return z_in[side, dest, chunk]

    def z_step(step):
        stage, chunk = step // chunks, step % chunks
        dest = target(stage)
        up = dest > z
        side = jnp.where(up, 0, 1)
        offset = PAIR * ((dest - z + depth) % depth)
        z_out[stage, chunk] = partial(offset, chunk)

        @pl.when(jnp.logical_or(x == 0, stage != skipped))
        def _():
            x_copy(stage, chunk).wait_recv()
            z_out[stage, chunk] = z_out[stage, chunk] + x_in[stage, chunk]

        @pl.when(jnp.where(up, z, depth - 1 - z) > 0)
        def _():
            z_out[stage, chunk] = z_out[stage, chunk] + arrived(side, dest, chunk)

        z_copy(side, dest, chunk, stage, jnp.where(up, site + PAIR, site - PAIR)).start()

    def field_copy(chunk):
        rows = pl.ds(pl.multiple_of(chunk * ROWS, ROWS), ROWS)
        return pltpu.make_async_copy(field.at[chunk], field_out.at[rows, :], f_send.at[chunk])

    def last_step(chunk):
        spare = z_out.at[stages, 0]
        spare[...] = partial(0, chunk)

        @pl.when(x == 1)
        def _():
            x_copy(stages, chunk).wait_recv()
            spare[...] = spare[...] + x_in[stages, chunk]

        @pl.when(z > 0)
        def _():
            spare[...] = spare[...] + arrived(0, z, chunk)

        @pl.when(z < depth - 1)
        def _():
            spare[...] = spare[...] + arrived(1, z, chunk)

        rounded = spare[...].astype(jnp.bfloat16)
        rows = pl.ds(pl.multiple_of(chunk * ROWS, ROWS), ROWS)
        field[chunk] = rounded
        field_copy(chunk).start()
        folded = None
        for piece in range(own_reals // LANES):
            residual = rounded[:, piece * LANES:(piece + 1) * LANES].astype(jnp.float32)
            log_peak = columns[0, rows, :] + columns[1, rows, :] * residual
            log_ratio = columns[2, rows, :] - log_peak
            margin = jnp.maximum(1.0 - jnp.exp(log_ratio), 0.0)
            displacement = coeff_disp * jnp.exp(power_margin * jnp.log(margin) - power_ratio * log_ratio)
            damage = jnp.log1p(displacement)
            folded = damage if folded is None else folded + damage
        folds[rows, :] = folded

        @pl.when((chunk + 1) % (LANES // ROWS) == 0)
        def _():
            line = chunk // (LANES // ROWS)
            group = folds[pl.ds(pl.multiple_of(line * LANES, LANES), LANES), :]
            totals[me, pl.ds(line, 1), :] = jnp.sum(group.T, axis=0, keepdims=True)

    for step in range(HEAD):
        x_step(step, head)
    for load in rest:
        load.wait()

    @pl.loop(HEAD, AHEAD)
    def _(step):
        x_step(step)

    @pl.loop(0, steps)
    def _(step):
        @pl.when(step + AHEAD < steps)
        def _():
            x_step(step + AHEAD)

        z_step(step)

        @pl.when(step < panels * tile // LANES)
        def _():
            spot = pl.ds(pl.multiple_of(step * LANES, LANES), LANES)
            for index, ref in enumerate((median, spread, critical)):
                value = ref[pl.ds(step, 1), :]
                value = jnp.log(value) if index == 2 else value
                columns[index, spot, :] = jnp.broadcast_to(value, (LANES, LANES)).T

        @pl.when(step >= steps - chunks + LAG)
        def _():
            last_step(step - (steps - chunks + LAG))

    @pl.loop(chunks - LAG, chunks)
    def _(chunk):
        last_step(chunk)

    def t_copy(shift):
        return pltpu.make_async_remote_copy(
            src_ref=totals.at[me],
            dst_ref=totals.at[me],
            send_sem=t_send.at[shift],
            recv_sem=t_recv.at[shift],
            device_id={"real": (me + shift) % reals},
            device_id_type=MESH,
        )

    for shift in range(1, reals):
        t_copy(shift).start()

    @pl.loop(0, steps)
    def _(step):
        x_copy(group_of(step // chunks), step % chunks).wait_send()
        z_copy(0, 0, step % chunks, step // chunks, (site + PAIR) % (PAIR * depth)).wait_send()

    @pl.loop(0, chunks)
    def _(chunk):
        field_copy(chunk).wait()

    for shift in range(1, reals):
        t_copy(shift).wait()
    total = totals[0]
    for source in range(1, reals):
        total = total + totals[source]
    mean_out[...] = total / (own_reals * reals)


def hand_out_kernel(field_in, mean_in, field_out, mean_out, field, mean, in_sem, out_sem):
    part = field.shape[1]
    reads = [pltpu.make_async_copy(mean_in, mean, in_sem.at[PARTS])]
    writes = [pltpu.make_async_copy(mean, mean_out, out_sem.at[PARTS])]
    for index in range(PARTS):
        rows = pl.ds(index * part, part)
        reads.append(pltpu.make_async_copy(field_in.at[rows, :], field.at[index], in_sem.at[index]))
        writes.append(pltpu.make_async_copy(field.at[index], field_out.at[rows, :], out_sem.at[index]))
    for read in reads:
        read.start()
    for read, write in zip(reads, writes):
        read.wait()
        write.start()
    for write in writes:
        write.wait()


def line_shards(epsilon, factor, block_rows, median_log, spread_log, critical_yield):
    panels, per_column, tile = factor.shape[:3]
    sites, own_reals = epsilon.shape
    count, reals = lax.axis_size("site"), lax.axis_size("real")
    depth = count // PAIR
    chunks = sites // ROWS
    lines = sites // LANES
    piece = (ROWS, own_reals)
    vmem = pl.BlockSpec(memory_space=pltpu.VMEM)
    anywhere = pl.BlockSpec(memory_space=pl.ANY)
    field, mean = pl.pallas_call(
        functools.partial(field_kernel, depth, own_reals),
        out_shape=(
            jax.ShapeDtypeStruct((sites, own_reals), jnp.bfloat16),
            jax.ShapeDtypeStruct((lines, LANES), jnp.float32),
        ),
        in_specs=[pl.BlockSpec(memory_space=pltpu.SMEM), anywhere, anywhere, vmem, vmem, vmem],
        out_specs=(anywhere, vmem),
        scratch_shapes=[
            pltpu.VMEM(epsilon.shape, epsilon.dtype),
            pltpu.VMEM(factor.shape, factor.dtype),
            pltpu.VMEM((panels, per_column, HEAD * ROWS, tile), factor.dtype),
            pltpu.VMEM((depth, chunks) + piece, jnp.float32),
            pltpu.VMEM((depth, chunks) + piece, jnp.float32),
            pltpu.VMEM((depth, chunks) + piece, jnp.float32),
            pltpu.VMEM((2, depth, chunks) + piece, jnp.float32),
            pltpu.VMEM((reals, lines, LANES), jnp.float32),
            pltpu.VMEM((3, sites, LANES), jnp.float32),
            pltpu.VMEM((sites, LANES), jnp.float32),
            pltpu.SMEM((2 * panels, (BAND // 2 + 1) * panels), jnp.int32),
            pltpu.VMEM((chunks, ROWS, own_reals), jnp.bfloat16),
            pltpu.SemaphoreType.DMA((1 + 2 * panels,)),
            pltpu.SemaphoreType.DMA((depth, chunks)),
            pltpu.SemaphoreType.DMA((depth, chunks)),
            pltpu.SemaphoreType.DMA((depth, chunks)),
            pltpu.SemaphoreType.DMA((2, depth, chunks)),
            pltpu.SemaphoreType.DMA((reals,)),
            pltpu.SemaphoreType.DMA((reals,)),
            pltpu.SemaphoreType.DMA((chunks,)),
        ],
        compiler_params=pltpu.CompilerParams(
            collective_id=0, has_side_effects=True, vmem_limit_bytes=60 * 1024 * 1024
        ),
    )(
        block_rows,
        epsilon,
        factor,
        median_log.reshape(lines, LANES),
        spread_log.reshape(lines, LANES),
        critical_yield.reshape(lines, LANES),
    )
    field, mean = pl.pallas_call(
        hand_out_kernel,
        out_shape=(
            jax.ShapeDtypeStruct(field.shape, field.dtype),
            jax.ShapeDtypeStruct(mean.shape, mean.dtype),
        ),
        in_specs=[anywhere, anywhere],
        out_specs=(anywhere, anywhere),
        scratch_shapes=[
            pltpu.VMEM((PARTS, sites // PARTS, own_reals), field.dtype),
            pltpu.VMEM(mean.shape, mean.dtype),
            pltpu.SemaphoreType.DMA((PARTS + 1,)),
            pltpu.SemaphoreType.DMA((PARTS + 1,)),
        ],
    )(field, mean)
    return field, mean.reshape(sites)


def solution(mesh):
    body = line_shards if mesh.shape["site"] == BAND // 2 + PAIR else shards
    return jax.shard_map(
        body,
        mesh=mesh,
        in_specs=(
            P("site", "real"),
            P(None, "site", None, None),
            P(None, "site"),
            P("site"),
            P("site"),
            P("site"),
        ),
        out_specs=(P("site", "real"), P("site")),
        check_vma=False,
    )
```

profile of v0, /device:TPU:11, one launch (start us, length us, event | category | flops | bytes accessed | tf_op | source)
XLA Modules:
  0.0 157.0 jit_solution(4838917016042175453)
XLA Ops:
  0.6 154.4 %shard_map.77 = (bf16[1024,512]{1,0:T(8,128)(2,1)}, f32[8,128]{1,0:T(8,128)}) custom-call(s32[2,9]{1,0:T(2,128)} %block_rows.1, bf16[1024,512]{1,0:T(8,128)(2,1)} %eps_in.1, bf16[2,9,512,512]{3,2,1,0:T(8,128)(2,1)} %factor_in.1, f32[8,128]{1,0:T(8,128)} %bitcast.4, f32[8,128]{1,0:T(8,128)} %bitcast.5, f32[8,128]{1,0:T(8,128)} %bitcast.6), custom_call_target="tpu_custom_call" | custom-call | tf_op jit(solution)/shard_map/pallas_call | solution.py:335
  155.0 2.0 %shard_map.78 = (bf16[1024,512]{1,0:T(8,128)(2,1)}, f32[8,128]{1,0:T(8,128)}) custom-call(bf16[1024,512]{1,0:T(8,128)(2,1)} %get-tuple-element.6.field_in, f32[8,128]{1,0:T(8,128)} %get-tuple-element.7.mean_in), custom_call_target="tpu_custom_call" | custom-call | tf_op jit(solution)/shard_map/pallas_call | solution.py:376
where the time goes:
time: 159 us; the launch traced here: 157 us
  Pallas kernels  156 us (98%)
    pallas_call x1, Pallas kernels, line_shards(): pl.pallas_call(functools.partial(field_kernel, depth, own_reals), out_sha...  154 us

commit v1 on v0

--- a/solution.py
+++ b/solution.py
@@ -10,10 +10,11 @@
 PAIR = 2
 LANES = 128
 ROWS = 64
-AHEAD = 6
 PARTS = 4
 HEAD = 2
-LAG = 1
+SITE_TILES = 16
+LAST_OFFSET = 12
+CROSS, UP, DOWN, KEEP = range(4)
 MESH = pl.DeviceIdType.MESH
 
 coeff_disp = 10.0**0.215
@@ -63,27 +64,179 @@
     mean_damage = total / (own_reals * lax.axis_size("real"))
     return (residual_field, mean_damage)
 
+LEFT, RIGHT, BOTH = (0,), (1,), (0, 1)
+ROUTES = {
+    0: [({}, {3: LEFT, 2: BOTH, 1: LEFT})] * 2,
+    1: [({}, {3: LEFT, 2: BOTH, 1: LEFT})] * 2,
+    2: [({}, {3: RIGHT, 2: RIGHT, 1: RIGHT})] * 2,
+    3: [({}, {3: RIGHT, 2: RIGHT, 1: RIGHT})] * 2,
+    4: [({0: LEFT}, {3: LEFT, 2: LEFT})] * 2,
+    5: [({0: LEFT}, {3: LEFT, 2: LEFT})] * 2,
+    6: [({0: RIGHT}, {3: RIGHT, 2: RIGHT})] * 2,
+    7: [({0: LEFT}, {3: LEFT, 2: LEFT}), ({0: RIGHT}, {3: RIGHT, 2: RIGHT})],
+    8: [({0: LEFT, 1: LEFT}, {3: LEFT})] * 2,
+    9: [({0: LEFT, 1: BOTH}, {3: RIGHT})] * 2,
+    10: [({0: RIGHT, 1: RIGHT}, {3: RIGHT})] * 2,
+    11: [({0: RIGHT, 1: RIGHT}, {})] * 2,
+    12: [({0: LEFT, 1: LEFT, 2: LEFT}, {})] * 2,
+    13: [({0: RIGHT, 1: LEFT, 2: LEFT}, {})] * 2,
+    14: [({0: RIGHT, 1: RIGHT, 2: RIGHT}, {})] * 2,
+    15: [({1: BOTH, 2: BOTH}, {})] * 2,
+}
+
+PLAN = {
+    (0, 0): (
+        (1, [4, 6, 13, 22, 15, 20, 21, 5, -1, 23, 12, -1, 7]),
+        (7, [9, 24, 8, 25, 18, 10, -1, -1, 19, 16, 14, 17, 11]),
+        (0, []),
+        (23, [1, -1, -1, -1, -1, -1, 2, 3, 0]),
+    ),
+    (0, 1): (
+        (3, [9, 24, 8, 25, 18, 10, -1, 19, 16, 14, 17, 11]),
+        (4, [29, 27, 28, 26, 22, -1, 20, 21, 15, 23, 13, 12]),
+        (0, []),
+        (27, [4, -1, -1, -1, -1, 6, 5, -1, 7]),
+    ),
+    (1, 0): (
+        (4, [13, 23, 29, 28, 21, 22, 12, 15, 20, -1, -1, 14]),
+        (10, [31, 30, 27, 24, 18, 25, 26, 19, 16, -1, 17]),
+        (16, [1, -1, -1, -1, -1, -1, 2, 3, 0]),
+        (38, [9, 8, -1, -1, 10, 11]),
+    ),
+    (1, 1): (
+        (4, [24, 1, 27, 2, 25, 26, 3, 16, 0, 17]),
+        (3, [18, 19, 31, 29, -1, 22, 30, 28, 21, 20, 23]),
+        (20, [4, -1, 5, -1, 7, 6]),
+        (39, [15, 14, 13, 12]),
+    ),
+    (2, 0): (
+        (0, [22, 4, -1, 29, 5, 7, 6, 21, 20, -1, 28, 23]),
+        (13, [31, -1, 30, 24, -1, -1, 27, -1, 25, 26]),
+        (15, [1, 0, 2, 11, 3, 9, 8, 14, 10]),
+        (35, [18, -1, -1, 19, 17, 16]),
+    ),
+    (2, 1): (
+        (3, [9, 8, 11, 24, 25, 18, -1, 27, 10, 26, -1, 19]),
+        (16, [31, -1, 29, -1, -1, -1, 30, 28]),
+        (0, [1, 0, 3, -1, 2, 4, 5, 6, -1, 15, 7, 12, 13]),
+        (43, [22, 21, 20, 23]),
+    ),
+    (3, 0): (
+        (0, [4, -1, -1, 15, 6, 5, 31, 12, 7, 30, 13, 28, 29]),
+        (0, []),
+        (10, [11, 1, 0, 2, 8, 3, 9, 14, 10, 17, 16]),
+        (31, [24, -1, -1, -1, 27, 25, 26]),
+    ),
+    (3, 1): (
+        (3, [11, -1, 1, -1, 0, 2, 8, 3, 9, 14, 10, 17, 16]),
+        (0, []),
+        (8, [18, 4, -1, 15, 6, 5, 19, 12, 7, 21, 13, 20]),
+        (34, [31, -1, -1, -1, 30, 29, 28]),
+    ),
+}
+
+
+def device_steps(depth, panels):
+    steps = {(z, x): {} for z in range(depth) for x in range(PAIR)}
+
+    def plane(z, unit, leaves, onward, arriving):
+        own = [(unit // 2 - panels * (PAIR * z + x)) % SITE_TILES <= LAST_OFFSET for x in range(PAIR)]
+        held = [x for x in range(PAIR) if own[x] or arriving.get(x)]
+        for x in held:
+            if x not in leaves:
+                steps[z, x][unit] = (own[x], tuple(arriving.get(x, ())), CROSS)
+        crossed = (CROSS,) if any(x not in leaves for x in held) else ()
+        for x in leaves:
+            steps[z, x][unit] = (own[x], tuple(arriving.get(x, ())) + crossed, onward)
+
+    for row, halves in ROUTES.items():
+        home, column = row // (panels * PAIR), row // panels % PAIR
+        for half, (rising, falling) in enumerate(halves):
+            unit, merged = 2 * row + half, {}
+            for onward, path, planes in ((UP, rising, range(home)), (DOWN, falling, range(depth - 1, home, -1))):
+                arriving = {}
+                for z in planes:
+                    if z in path:
+                        plane(z, unit, path[z], onward, arriving)
+                        arriving = {x: (onward,) for x in path[z]}
+                for x, kinds in arriving.items():
+                    merged[x] = merged.get(x, ()) + kinds
+            plane(home, unit, (column,), KEEP, merged)
+    return steps
+
+
+def stream_words(depth, panels):
+    steps = device_steps(depth, panels)
+
+    def target(device, way):
+        z, x = device
+        return {CROSS: (z, 1 - x), UP: (z + 1, x), DOWN: (z - 1, x)}[way]
+
+    bases = {}
+    for device, streams in PLAN.items():
+        for way in (CROSS, UP, DOWN):
+            sent = [unit for unit in streams[way][1] if unit >= 0]
+            assert all(steps[device][unit][2] == way for unit in sent)
+            for base, unit in enumerate(sent):
+                bases[target(device, way), unit, way] = base
+    words = {}
+    for device, streams in PLAN.items():
+        planned = [unit for stream in streams for unit in stream[1] if unit >= 0]
+        assert sorted(planned) == sorted(steps[device])
+        first, words[device] = panels * (PAIR * device[0] + device[1]), []
+        for way, (start, units) in enumerate(streams):
+            line = []
+            for unit in units:
+                if unit < 0:
+                    line.append(0)
+                    continue
+                own, arriving, onward = steps[device][unit]
+                assert onward == way
+                base = 0 if way == KEEP else bases[target(device, way), unit, way]
+                word = 1 + 2 * ((unit - 2 * first) % (2 * SITE_TILES)) + 64 * base
+                for kind in arriving:
+                    word += (1 + 2 * bases[device, unit, kind]) * 1024 * 32**kind
+                line.append(word)
+            words[device].append((start, line))
+        own, arriving, _ = steps[device][streams[CROSS][1][0]]
+        assert own and not arriving
+    return words
+
 
 def field_kernel(
-    depth, own_reals, block_rows, eps_in, factor_in, median, spread, critical, field_out, mean_out,
-    eps, factor, head, x_out, x_in, z_out, z_in, totals, columns, folds, table, field,
-    load_sem, x_send, x_recv, z_send, z_recv, t_send, t_recv, f_send,
+    words, own_reals, block_rows, eps_in, factor_in, median, spread, critical, field_out, mean_out,
+    eps, factor, head, x_out, u_out, d_out, x_in, u_in, d_in, spare, totals, columns, folds, table, field,
+    load_sem, x_send, u_send, d_send, x_recv, u_recv, d_recv, t_send, t_recv, f_send,
 ):
     panels, per_column, tile = factor.shape[0], factor.shape[1], factor.shape[2]
+    depth = len(words) // PAIR
+    count = PAIR * depth
     chunks = panels * tile // ROWS
     per_tile = tile // ROWS
-    stages = depth - 1
-    steps = stages * chunks
+    per_unit = per_tile // 2
+    lines = panels * tile // LANES
     reals = lax.axis_size("real")
     site = lax.axis_index("site")
     me = lax.axis_index("real")
     z, x = site // PAIR, site % PAIR
-
+    here = {device: site == device[0] * PAIR + device[1] for device in words}
+
+    def pick(values):
+        result = None
+        for device, value in values.items():
+            value = jnp.int32(value)
+            result = value if result is None else jnp.where(here[device], value, result)
+        return result
+
+    begin = pick({
+        device: (own[CROSS][1][0] // 2 % 2) * (tile // 2) for device, own in words.items()
+    })
     first = [pltpu.make_async_copy(eps_in, eps, load_sem.at[0])]
     rest = []
     for panel in range(panels):
         first.append(pltpu.make_async_copy(
-            factor_in.at[panel, :, :head.shape[2], :], head.at[panel], load_sem.at[1 + panel]
+            factor_in.at[panel, :, pl.ds(pl.multiple_of(begin, tile // 2), head.shape[2]), :],
+            head.at[panel], load_sem.at[1 + panel],
         ))
         rest.append(pltpu.make_async_copy(
             factor_in.at[panel], factor.at[panel], load_sem.at[1 + panels + panel]
@@ -104,9 +257,22 @@
     def _():
         pl.semaphore_signal(barrier, inc=1, device_id={"site": site + PAIR}, device_id_type=MESH)
 
+    plan, starts, sent, slots = [], [], [], 0
+    for way in range(4):
+        longest = max(len(own[way][1]) for own in words.values())
+        plan.append([
+            pick({device: (own[way][1] + [0] * longest)[number] for device, own in words.items()})
+            for number in range(longest)
+        ])
+        starts.append(pick({device: own[way][0] for device, own in words.items()}))
+        sent.append(pick({
+            device: per_unit * sum(word > 0 for word in own[way][1]) for device, own in words.items()
+        }))
+        slots = max([slots] + [own[way][0] + per_unit * len(own[way][1]) for own in words.values()])
+
     for panel in range(panels):
         begins = [
-            (block_rows[panel, block] - site * panels + panels * PAIR * depth) % (panels * PAIR * depth)
+            (block_rows[panel, block] - site * panels + panels * count) % (panels * count)
             for block in range(per_column)
         ]
 
@@ -125,102 +291,48 @@
     for load in first:
         load.wait()
 
-    def partial(offset, chunk, source=factor):
-        relative = panels * offset + chunk // per_tile
-        row = pl.multiple_of((chunk % per_tile) * ROWS, ROWS)
-        result = None
-        for panel in range(panels):
-            block = source[panel, table[panel, relative], pl.ds(row, ROWS), :]
-            product = jnp.dot(
-                block, eps[panel * tile:(panel + 1) * tile, :], preferred_element_type=jnp.float32
-            ) * table[panels + panel, relative].astype(jnp.float32)
-            result = product if result is None else result + product
-        return result
-
-    low = 2 * z < depth
-
-    def target(stage):
-        falling = depth - 1 - stage
-        of_low = jnp.where(falling > z, falling, stage - (depth - 1 - z))
-        of_high = jnp.where(stage < z, stage, depth - 1 - (stage - z))
-        of_stage = jnp.where(low, of_low, of_high)
-        return jnp.where(stage == stages, z, of_stage)
-
-    skipped = jnp.where(z == 0, 0, jnp.where(low, stages - 1, z - 1))
-
-    def x_copy(group, chunk):
+    def bits(word, low, width):
+        return lax.rem(lax.div(word, jnp.int32(2**low)), jnp.int32(2**width))
+
+    def multiply(out, relative, piece, source):
+        @pl.when(relative <= LAST_OFFSET)
+        def _():
+            row = pl.multiple_of(piece * ROWS, ROWS)
+            result = None
+            for panel in range(panels):
+                block = source[panel, table[panel, relative], pl.ds(row, ROWS), :]
+                product = jnp.dot(
+                    block, eps[panel * tile:(panel + 1) * tile, :], preferred_element_type=jnp.float32
+                ) * table[panels + panel, relative].astype(jnp.float32)
+                result = product if result is None else result + product
+            out[...] = result
+
+        @pl.when(relative > LAST_OFFSET)
+        def _():
+            out[...] = jnp.zeros_like(out)
+
+    ways = (
+        (x_out, x_in, x_send, x_recv, site + 1 - 2 * x),
+        (u_out, u_in, u_send, u_recv, (site + PAIR) % count),
+        (d_out, d_in, d_send, d_recv, (site + count - PAIR) % count),
+    )
+
+    def copy(way, slot):
+        leaving, landing, departure, arrival, there = ways[way]
         return pltpu.make_async_remote_copy(
-            src_ref=x_out.at[group, chunk],
-            dst_ref=x_in.at[group, chunk],
-            send_sem=x_send.at[group, chunk],
-            recv_sem=x_recv.at[group, chunk],
-            device_id={"site": site + 1 - 2 * x},
-            device_id_type=MESH,
-        )
-
-    def group_of(turn):
-        return jnp.where(x == 0, jnp.where(turn >= skipped, turn + 1, turn), turn)
-
-    def x_step(step, source=factor):
-        group, chunk = group_of(step // chunks), step % chunks
-        offset = (PAIR * (target(group) - z + depth) + 1 - 2 * x) % (PAIR * depth)
-        x_out[group, chunk] = partial(offset, chunk, source)
-        x_copy(group, chunk).start()
-
-    def z_copy(side, dest, chunk, stage, there):
-        return pltpu.make_async_remote_copy(
-            src_ref=z_out.at[stage, chunk],
-            dst_ref=z_in.at[side, dest, chunk],
-            send_sem=z_send.at[stage, chunk],
-            recv_sem=z_recv.at[side, dest, chunk],
+            src_ref=leaving.at[slot],
+            dst_ref=landing.at[slot],
+            send_sem=departure.at[slot],
+            recv_sem=arrival.at[slot],
             device_id={"site": there},
             device_id_type=MESH,
         )
 
-    def arrived(side, dest, chunk):
-        z_copy(side, dest, chunk, 0, (site + PAIR) % (PAIR * depth)).wait_recv()
-        return z_in[side, dest, chunk]
-
-    def z_step(step):
-        stage, chunk = step // chunks, step % chunks
-        dest = target(stage)
-        up = dest > z
-        side = jnp.where(up, 0, 1)
-        offset = PAIR * ((dest - z + depth) % depth)
-        z_out[stage, chunk] = partial(offset, chunk)
-
-        @pl.when(jnp.logical_or(x == 0, stage != skipped))
-        def _():
-            x_copy(stage, chunk).wait_recv()
-            z_out[stage, chunk] = z_out[stage, chunk] + x_in[stage, chunk]
-
-        @pl.when(jnp.where(up, z, depth - 1 - z) > 0)
-        def _():
-            z_out[stage, chunk] = z_out[stage, chunk] + arrived(side, dest, chunk)
-
-        z_copy(side, dest, chunk, stage, jnp.where(up, site + PAIR, site - PAIR)).start()
-
     def field_copy(chunk):
         rows = pl.ds(pl.multiple_of(chunk * ROWS, ROWS), ROWS)
         return pltpu.make_async_copy(field.at[chunk], field_out.at[rows, :], f_send.at[chunk])
 
-    def last_step(chunk):
-        spare = z_out.at[stages, 0]
-        spare[...] = partial(0, chunk)
-
-        @pl.when(x == 1)
-        def _():
-            x_copy(stages, chunk).wait_recv()
-            spare[...] = spare[...] + x_in[stages, chunk]
-
-        @pl.when(z > 0)
-        def _():
-            spare[...] = spare[...] + arrived(0, z, chunk)
-
-        @pl.when(z < depth - 1)
-        def _():
-            spare[...] = spare[...] + arrived(1, z, chunk)
-
+    def keep(chunk):
         rounded = spare[...].astype(jnp.bfloat16)
         rows = pl.ds(pl.multiple_of(chunk * ROWS, ROWS), ROWS)
         field[chunk] = rounded
@@ -242,38 +354,55 @@
             group = folds[pl.ds(pl.multiple_of(line * LANES, LANES), LANES), :]
             totals[me, pl.ds(line, 1), :] = jnp.sum(group.T, axis=0, keepdims=True)
 
-    for step in range(HEAD):
-        x_step(step, head)
+    def step(way, slot, source, least=0):
+        number = slot - starts[way] + per_unit * slots
+        group = lax.div(number, jnp.int32(per_unit)) - slots
+        turn = lax.rem(number, jnp.int32(per_unit))
+        word = jnp.int32(0)
+        for index, value in enumerate(plan[way]):
+            word = jnp.where(group == index, value, word)
+
+        @pl.when(jnp.logical_and(word > 0, slot - starts[way] >= least))
+        def _():
+            relative = bits(word, 2, 4)
+            piece = bits(word, 1, 1) * per_unit + turn
+            place = bits(word, 6, 4) * per_unit + turn
+            out = spare if way == KEEP else ways[way][0].at[place]
+            multiply(out, relative, piece if source is factor else turn, source)
+            if source is not factor:
+                copy(way, place).start()
+                return
+            for kind in range(3):
+                @pl.when(bits(word, 10 + 5 * kind, 1) == 1)
+                def _():
+                    arrived = bits(word, 11 + 5 * kind, 4) * per_unit + turn
+                    copy(kind, arrived).wait_recv()
+                    out[...] = out[...] + ways[kind][1][arrived]
+
+            if way == KEEP:
+                keep(relative * per_tile + piece)
+            else:
+                copy(way, place).start()
+
+    for slot in range(HEAD):
+        step(CROSS, starts[CROSS] + slot, head)
     for load in rest:
         load.wait()
 
-    @pl.loop(HEAD, AHEAD)
-    def _(step):
-        x_step(step)
-
-    @pl.loop(0, steps)
-    def _(step):
-        @pl.when(step + AHEAD < steps)
+    @pl.loop(0, slots)
+    def _(slot):
+        step(CROSS, slot, factor, HEAD)
+
+        @pl.when(slot < lines)
         def _():
-            x_step(step + AHEAD)
-
-        z_step(step)
-
-        @pl.when(step < panels * tile // LANES)
-        def _():
-            spot = pl.ds(pl.multiple_of(step * LANES, LANES), LANES)
+            spot = pl.ds(pl.multiple_of(slot * LANES, LANES), LANES)
             for index, ref in enumerate((median, spread, critical)):
-                value = ref[pl.ds(step, 1), :]
+                value = ref[pl.ds(slot, 1), :]
                 value = jnp.log(value) if index == 2 else value
                 columns[index, spot, :] = jnp.broadcast_to(value, (LANES, LANES)).T
 
-        @pl.when(step >= steps - chunks + LAG)
-        def _():
-            last_step(step - (steps - chunks + LAG))
-
-    @pl.loop(chunks - LAG, chunks)
-    def _(chunk):
-        last_step(chunk)
+        for way in (UP, DOWN, KEEP):
+            step(way, slot, factor)
 
     def t_copy(shift):
         return pltpu.make_async_remote_copy(
@@ -288,10 +417,10 @@
     for shift in range(1, reals):
         t_copy(shift).start()
 
-    @pl.loop(0, steps)
-    def _(step):
-        x_copy(group_of(step // chunks), step % chunks).wait_send()
-        z_copy(0, 0, step % chunks, step // chunks, (site + PAIR) % (PAIR * depth)).wait_send()
+    for way in (CROSS, UP, DOWN):
+        @pl.loop(0, sent[way])
+        def _(slot):
+            copy(way, slot).wait_send()
 
     @pl.loop(0, chunks)
     def _(chunk):
@@ -326,14 +455,18 @@
     panels, per_column, tile = factor.shape[:3]
     sites, own_reals = epsilon.shape
     count, reals = lax.axis_size("site"), lax.axis_size("real")
-    depth = count // PAIR
     chunks = sites // ROWS
     lines = sites // LANES
+    words = stream_words(count // PAIR, panels)
+    most = [
+        max(sum(word > 0 for word in own[way][1]) for own in words.values()) * (tile // ROWS // 2)
+        for way in (CROSS, UP, DOWN)
+    ]
     piece = (ROWS, own_reals)
     vmem = pl.BlockSpec(memory_space=pltpu.VMEM)
     anywhere = pl.BlockSpec(memory_space=pl.ANY)
     field, mean = pl.pallas_call(
-        functools.partial(field_kernel, depth, own_reals),
+        functools.partial(field_kernel, words, own_reals),
         out_shape=(
             jax.ShapeDtypeStruct((sites, own_reals), jnp.bfloat16),
             jax.ShapeDtypeStruct((lines, LANES), jnp.float32),
@@ -344,20 +477,15 @@
             pltpu.VMEM(epsilon.shape, epsilon.dtype),
             pltpu.VMEM(factor.shape, factor.dtype),
             pltpu.VMEM((panels, per_column, HEAD * ROWS, tile), factor.dtype),
-            pltpu.VMEM((depth, chunks) + piece, jnp.float32),
-            pltpu.VMEM((depth, chunks) + piece, jnp.float32),
-            pltpu.VMEM((depth, chunks) + piece, jnp.float32),
-            pltpu.VMEM((2, depth, chunks) + piece, jnp.float32),
+            *[pltpu.VMEM((slots,) + piece, jnp.float32) for slots in most + most],
+            pltpu.VMEM(piece, jnp.float32),
             pltpu.VMEM((reals, lines, LANES), jnp.float32),
             pltpu.VMEM((3, sites, LANES), jnp.float32),
             pltpu.VMEM((sites, LANES), jnp.float32),
-            pltpu.SMEM((2 * panels, (BAND // 2 + 1) * panels), jnp.int32),
+            pltpu.SMEM((2 * panels, SITE_TILES), jnp.int32),
             pltpu.VMEM((chunks, ROWS, own_reals), jnp.bfloat16),
             pltpu.SemaphoreType.DMA((1 + 2 * panels,)),
-            pltpu.SemaphoreType.DMA((depth, chunks)),
-            pltpu.SemaphoreType.DMA((depth, chunks)),
-            pltpu.SemaphoreType.DMA((depth, chunks)),
-            pltpu.SemaphoreType.DMA((2, depth, chunks)),
+            *[pltpu.SemaphoreType.DMA((slots,)) for slots in most + most],
             pltpu.SemaphoreType.DMA((reals,)),
             pltpu.SemaphoreType.DMA((reals,)),
             pltpu.SemaphoreType.DMA((chunks,)),

time: 159 us -> 147 us (0.925)
  Pallas kernels: 156 us -> 144 us
    pallas_call x1, Pallas kernels: 154 us -> 142 us  [line_shards(): pl.pallas_call(functools.partial(field_kernel, words, own_reals), out_sha...]
where the time goes in v1:
time: 147 us; the launch traced here: 145 us
  Pallas kernels  144 us (98%)
    pallas_call x1, Pallas kernels, line_shards(): pl.pallas_call(functools.partial(field_kernel, words, own_reals), out_sha...  142 us

profile of v1, /device:TPU:11, one launch (start us, length us, event | category | flops | bytes accessed | tf_op | source)
XLA Modules:
  0.0 144.7 jit_solution(13385944188968762512)
XLA Ops:
  0.6 142.1 %shard_map.77 = (bf16[1024,512]{1,0:T(8,128)(2,1)}, f32[8,128]{1,0:T(8,128)}) custom-call(s32[2,9]{1,0:T(2,128)} %block_rows.1, bf16[1024,512]{1,0:T(8,128)(2,1)} %eps_in.1, bf16[2,9,512,512]{3,2,1,0:T(8,128)(2,1)} %factor_in.1, f32[8,128]{1,0:T(8,128)} %bitcast.4, f32[8,128]{1,0:T(8,128)} %bitcast.5, f32[8,128]{1,0:T(8,128)} %bitcast.6), custom_call_target="tpu_custom_call" | custom-call | tf_op jit(solution)/shard_map/pallas_call | solution.py:468
  142.7 2.0 %shard_map.78 = (bf16[1024,512]{1,0:T(8,128)(2,1)}, f32[8,128]{1,0:T(8,128)}) custom-call(bf16[1024,512]{1,0:T(8,128)(2,1)} %get-tuple-element.6.field_in, f32[8,128]{1,0:T(8,128)} %get-tuple-element.7.mean_in), custom_call_target="tpu_custom_call" | custom-call | tf_op jit(solution)/shard_map/pallas_call | solution.py:504

commit v2 on v1

--- a/solution.py
+++ b/solution.py
@@ -84,56 +84,63 @@
     15: [({1: BOTH, 2: BOTH}, {})] * 2,
 }
 
+SPLITS = {7: 3}
+
 PLAN = {
     (0, 0): (
-        (1, [4, 6, 13, 22, 15, 20, 21, 5, -1, 23, 12, -1, 7]),
-        (7, [9, 24, 8, 25, 18, 10, -1, -1, 19, 16, 14, 17, 11]),
-        (0, []),
-        (23, [1, -1, -1, -1, -1, -1, 2, 3, 0]),
+        [(0, 22), (4, 23), (10, 12), (14, 13), (18, 6), (23, 20), (27, 4), (35, 21), (42, 15), (49, 5), (54, 7)],
+        [(2, 14), (6, 9), (13, 25), (17, 19), (24, 24), (29, 10), (33, 18), (39, 17), (43, 8), (49, 16), (56, 11)],
+        [],
+        [(31, 2), (44, 3), (48, 0), (56, 1)],
     ),
     (0, 1): (
-        (3, [9, 24, 8, 25, 18, 10, -1, 19, 16, 14, 17, 11]),
-        (4, [29, 27, 28, 26, 22, -1, 20, 21, 15, 23, 13, 12]),
-        (0, []),
-        (27, [4, -1, -1, -1, -1, 6, 5, -1, 7]),
+        [(0, 14), (5, 9), (9, 25), (13, 19), (20, 24), (26, 10), (30, 18), (34, 17), (42, 8), (48, 16), (52, 11)],
+        [(0, 29), (7, 26), (11, 28), (15, 22), (22, 13), (26, 23), (30, 12), (34, 27), (40, 20), (46, 21), (50, 15)],
+        [],
+        [(43, 4), (47, 6), (52, 5), (56, 7)],
     ),
     (1, 0): (
-        (4, [13, 23, 29, 28, 21, 22, 12, 15, 20, -1, -1, 14]),
-        (10, [31, 30, 27, 24, 18, 25, 26, 19, 16, -1, 17]),
-        (16, [1, -1, -1, -1, -1, -1, 2, 3, 0]),
-        (38, [9, 8, -1, -1, 10, 11]),
+        [(0, 28), (4, 13), (8, 22), (12, 23), (18, 20), (25, 29), (29, 14), (33, 12), (42, 21), (50, 15)],
+        [(1, 30), (5, 31), (10, 25), (14, 19), (18, 26), (24, 24), (28, 18), (39, 17), (44, 27), (51, 16)],
+        [(17, 2), (28, 0), (35, 3), (43, 1)],
+        [(39, 10), (45, 9), (49, 8), (53, 11)],
     ),
     (1, 1): (
-        (4, [24, 1, 27, 2, 25, 26, 3, 16, 0, 17]),
-        (3, [18, 19, 31, 29, -1, 22, 30, 28, 21, 20, 23]),
-        (20, [4, -1, 5, -1, 7, 6]),
-        (39, [15, 14, 13, 12]),
+        [(1, 17), (5, 2), (9, 25), (13, 24), (18, 26), (24, 0), (31, 3), (35, 1), (43, 27), (47, 16)],
+        [(0, 31), (5, 19), (10, 28), (16, 22), (22, 30), (28, 18), (35, 29), (41, 23), (45, 20), (55, 21)],
+        [(25, 4), (31, 6), (45, 5), (54, 7)],
+        [(35, 13), (39, 14), (51, 12), (56, 15)],
     ),
     (2, 0): (
-        (0, [22, 4, -1, 29, 5, 7, 6, 21, 20, -1, 28, 23]),
-        (13, [31, -1, 30, 24, -1, -1, 27, -1, 25, 26]),
-        (15, [1, 0, 2, 11, 3, 9, 8, 14, 10]),
-        (35, [18, -1, -1, 19, 17, 16]),
+        [(0, 6), (4, 4), (8, 22), (12, 28), (21, 5), (25, 7), (37, 29), (43, 23), (47, 21), (51, 20)],
+        [(10, 31), (14, 25), (26, 26), (33, 30), (37, 24), (53, 27)],
+        [(5, 0), (10, 2), (15, 14), (23, 1), (27, 3), (38, 10), (42, 9), (46, 8), (53, 11)],
+        [(47, 19), (51, 18), (55, 17), (59, 16)],
     ),
     (2, 1): (
-        (3, [9, 8, 11, 24, 25, 18, -1, 27, 10, 26, -1, 19]),
-        (16, [31, -1, 29, -1, -1, -1, 30, 28]),
-        (0, [1, 0, 3, -1, 2, 4, 5, 6, -1, 15, 7, 12, 13]),
-        (43, [22, 21, 20, 23]),
+        [(0, 26), (4, 24), (9, 25), (14, 9), (20, 10), (25, 8), (34, 27), (38, 19), (42, 11), (47, 18)],
+        [(16, 31), (37, 28), (43, 29), (47, 30)],
+        [(0, 0), (4, 2), (8, 1), (12, 3), (22, 6), (26, 4), (31, 13), (37, 12), (42, 5), (47, 7), (51, 15)],
+        [(43, 22), (47, 23), (52, 20), (56, 21)],
     ),
     (3, 0): (
-        (0, [4, -1, -1, 15, 6, 5, 31, 12, 7, 30, 13, 28, 29]),
-        (0, []),
-        (10, [11, 1, 0, 2, 8, 3, 9, 14, 10, 17, 16]),
-        (31, [24, -1, -1, -1, 27, 25, 26]),
+        [(0, 5), (4, 6), (9, 4), (13, 13), (17, 12), (24, 28), (29, 31), (35, 7), (40, 15), (47, 30), (53, 29)],
+        [],
+        [(3, 2), (7, 0), (12, 14), (16, 11), (22, 1), (27, 3), (34, 10), (40, 9), (46, 8), (50, 16), (54, 17)],
+        [(40, 26), (46, 24), (50, 25), (56, 27)],
     ),
     (3, 1): (
-        (3, [11, -1, 1, -1, 0, 2, 8, 3, 9, 14, 10, 17, 16]),
-        (0, []),
-        (8, [18, 4, -1, 15, 6, 5, 19, 12, 7, 21, 13, 20]),
-        (34, [31, -1, -1, -1, 30, 29, 28]),
+        [(0, 2), (4, 0), (8, 14), (13, 11), (19, 1), (23, 3), (27, 10), (32, 9), (36, 8), (44, 16), (50, 17)],
+        [],
+        [(0, 19), (4, 5), (8, 18), (20, 6), (24, 4), (29, 13), (33, 12), (39, 20), (43, 7), (47, 15), (54, 21)],
+        [(39, 31), (44, 28), (51, 30), (55, 29)],
     ),
 }
+
+
+def pieces(unit, per_tile):
+    cut = SPLITS.get(unit // 2, 4) * per_tile // 8
+    return (cut, per_tile - cut) if unit % 2 else (0, cut)
 
 
 def device_steps(depth, panels):
@@ -165,55 +172,54 @@
     return steps
 
 
-def stream_words(depth, panels):
+def stream_words(depth, panels, per_tile):
     steps = device_steps(depth, panels)
 
     def target(device, way):
         z, x = device
         return {CROSS: (z, 1 - x), UP: (z + 1, x), DOWN: (z - 1, x)}[way]
 
-    bases = {}
+    bases, sent = {}, {}
     for device, streams in PLAN.items():
         for way in (CROSS, UP, DOWN):
-            sent = [unit for unit in streams[way][1] if unit >= 0]
-            assert all(steps[device][unit][2] == way for unit in sent)
-            for base, unit in enumerate(sent):
+            base = 0
+            for _, unit in streams[way]:
+                assert steps[device][unit][2] == way
                 bases[target(device, way), unit, way] = base
+                base += pieces(unit, per_tile)[1]
+            sent[device, way] = base
     words = {}
     for device, streams in PLAN.items():
-        planned = [unit for stream in streams for unit in stream[1] if unit >= 0]
+        planned = [unit for stream in streams for _, unit in stream]
         assert sorted(planned) == sorted(steps[device])
-        first, words[device] = panels * (PAIR * device[0] + device[1]), []
-        for way, (start, units) in enumerate(streams):
-            line = []
-            for unit in units:
-                if unit < 0:
-                    line.append(0)
-                    continue
+        origin, words[device] = panels * (PAIR * device[0] + device[1]), []
+        for way, stream in enumerate(streams):
+            line, free = [], 0
+            for start, unit in stream:
                 own, arriving, onward = steps[device][unit]
-                assert onward == way
+                begin, length = pieces(unit, per_tile)
+                start = start * per_tile // 8
+                assert onward == way and start >= free
+                free = start + length
                 base = 0 if way == KEEP else bases[target(device, way), unit, way]
-                word = 1 + 2 * ((unit - 2 * first) % (2 * SITE_TILES)) + 64 * base
-                for kind in arriving:
-                    word += (1 + 2 * bases[device, unit, kind]) * 1024 * 32**kind
-                line.append(word)
-            words[device].append((start, line))
-        own, arriving, _ = steps[device][streams[CROSS][1][0]]
+                one = (unit // 2 - origin) % SITE_TILES + 16 * begin + 128 * base
+                two = sum((1 + 2 * bases[device, unit, kind]) * 128**kind for kind in arriving)
+                line.append((start, length, one, two))
+            words[device].append(line)
+        own, arriving, _ = steps[device][streams[CROSS][0][1]]
         assert own and not arriving
-    return words
+    return words, sent
 
 
 def field_kernel(
-    words, own_reals, block_rows, eps_in, factor_in, median, spread, critical, field_out, mean_out,
-    eps, factor, head, x_out, u_out, d_out, x_in, u_in, d_in, spare, totals, columns, folds, table, field,
-    load_sem, x_send, u_send, d_send, x_recv, u_recv, d_recv, t_send, t_recv, f_send,
+    words, sent, own_reals, block_rows, eps_in, factor_in, median, spread, critical, field, mean_out,
+    eps, factor, head, x_out, u_out, d_out, x_in, u_in, d_in, spare, totals, columns, folds, table,
+    load_sem, x_send, u_send, d_send, x_recv, u_recv, d_recv, t_send, t_recv,
 ):
     panels, per_column, tile = factor.shape[0], factor.shape[1], factor.shape[2]
     depth = len(words) // PAIR
     count = PAIR * depth
-    chunks = panels * tile // ROWS
     per_tile = tile // ROWS
-    per_unit = per_tile // 2
     lines = panels * tile // LANES
     reals = lax.axis_size("real")
     site = lax.axis_index("site")
@@ -228,14 +234,12 @@
             result = value if result is None else jnp.where(here[device], value, result)
         return result
 
-    begin = pick({
-        device: (own[CROSS][1][0] // 2 % 2) * (tile // 2) for device, own in words.items()
-    })
+    begin = pick({device: own[CROSS][0][2] // 16 % 8 * ROWS for device, own in words.items()})
     first = [pltpu.make_async_copy(eps_in, eps, load_sem.at[0])]
     rest = []
     for panel in range(panels):
         first.append(pltpu.make_async_copy(
-            factor_in.at[panel, :, pl.ds(pl.multiple_of(begin, tile // 2), head.shape[2]), :],
+            factor_in.at[panel, :, pl.ds(pl.multiple_of(begin, ROWS), head.shape[2]), :],
             head.at[panel], load_sem.at[1 + panel],
         ))
         rest.append(pltpu.make_async_copy(
@@ -257,18 +261,15 @@
     def _():
         pl.semaphore_signal(barrier, inc=1, device_id={"site": site + PAIR}, device_id_type=MESH)
 
-    plan, starts, sent, slots = [], [], [], 0
+    plan, slots = [], 0
     for way in range(4):
-        longest = max(len(own[way][1]) for own in words.values())
+        longest = max(len(own[way]) for own in words.values())
+        pad = [(2**20, 0, 0, 0)] * longest
         plan.append([
-            pick({device: (own[way][1] + [0] * longest)[number] for device, own in words.items()})
+            [pick({device: (own[way] + pad)[number][field] for device, own in words.items()}) for field in range(4)]
             for number in range(longest)
         ])
-        starts.append(pick({device: own[way][0] for device, own in words.items()}))
-        sent.append(pick({
-            device: per_unit * sum(word > 0 for word in own[way][1]) for device, own in words.items()
-        }))
-        slots = max([slots] + [own[way][0] + per_unit * len(own[way][1]) for own in words.values()])
+        slots = max([slots] + [own[way][-1][0] + own[way][-1][1] for own in words.values() if own[way]])
 
     for panel in range(panels):
         begins = [
@@ -285,11 +286,6 @@
                 found = jnp.where(hit, 1, found)
             table[panel, slot] = number
             table[panels + panel, slot] = found
-
-    pl.semaphore_wait(barrier, reals + jnp.where(z > 0, 1, 0) + jnp.where(z < depth - 1, 1, 0))
-
-    for load in first:
-        load.wait()
 
     def bits(word, low, width):
         return lax.rem(lax.div(word, jnp.int32(2**low)), jnp.int32(2**width))
@@ -328,15 +324,10 @@
             device_id_type=MESH,
         )
 
-    def field_copy(chunk):
-        rows = pl.ds(pl.multiple_of(chunk * ROWS, ROWS), ROWS)
-        return pltpu.make_async_copy(field.at[chunk], field_out.at[rows, :], f_send.at[chunk])
-
     def keep(chunk):
         rounded = spare[...].astype(jnp.bfloat16)
         rows = pl.ds(pl.multiple_of(chunk * ROWS, ROWS), ROWS)
-        field[chunk] = rounded
-        field_copy(chunk).start()
+        field[rows, :] = rounded
         folded = None
         for piece in range(own_reals // LANES):
             residual = rounded[:, piece * LANES:(piece + 1) * LANES].astype(jnp.float32)
@@ -354,28 +345,26 @@
             group = folds[pl.ds(pl.multiple_of(line * LANES, LANES), LANES), :]
             totals[me, pl.ds(line, 1), :] = jnp.sum(group.T, axis=0, keepdims=True)
 
-    def step(way, slot, source, least=0):
-        number = slot - starts[way] + per_unit * slots
-        group = lax.div(number, jnp.int32(per_unit)) - slots
-        turn = lax.rem(number, jnp.int32(per_unit))
-        word = jnp.int32(0)
-        for index, value in enumerate(plan[way]):
-            word = jnp.where(group == index, value, word)
-
-        @pl.when(jnp.logical_and(word > 0, slot - starts[way] >= least))
+    def step(way, slot, least=0):
+        turn, count, one, two = jnp.int32(0), jnp.int32(0), jnp.int32(0), jnp.int32(0)
+        for start, length, first_word, second_word in plan[way]:
+            later = slot >= start
+            turn = jnp.where(later, slot - start, turn)
+            count = jnp.where(later, length, count)
+            one = jnp.where(later, first_word, one)
+            two = jnp.where(later, second_word, two)
+
+        @pl.when(jnp.logical_and(turn < count, slot >= least))
         def _():
-            relative = bits(word, 2, 4)
-            piece = bits(word, 1, 1) * per_unit + turn
-            place = bits(word, 6, 4) * per_unit + turn
+            relative = bits(one, 0, 4)
+            piece = bits(one, 4, 3) + turn
+            place = bits(one, 7, 6) + turn
             out = spare if way == KEEP else ways[way][0].at[place]
-            multiply(out, relative, piece if source is factor else turn, source)
-            if source is not factor:
-                copy(way, place).start()
-                return
+            multiply(out, relative, piece, factor)
             for kind in range(3):
-                @pl.when(bits(word, 10 + 5 * kind, 1) == 1)
+                @pl.when(bits(two, 7 * kind, 1) == 1)
                 def _():
-                    arrived = bits(word, 11 + 5 * kind, 4) * per_unit + turn
+                    arrived = bits(two, 7 * kind + 1, 6) + turn
                     copy(kind, arrived).wait_recv()
                     out[...] = out[...] + ways[kind][1][arrived]
 
@@ -384,14 +373,19 @@
             else:
                 copy(way, place).start()
 
-    for slot in range(HEAD):
-        step(CROSS, starts[CROSS] + slot, head)
+    for load in first:
+        load.wait()
+    for turn in range(HEAD):
+        multiply(x_out.at[turn], bits(plan[CROSS][0][2], 0, 4), turn, head)
+    pl.semaphore_wait(barrier, reals + jnp.where(z > 0, 1, 0) + jnp.where(z < depth - 1, 1, 0))
+    for turn in range(HEAD):
+        copy(CROSS, turn).start()
     for load in rest:
         load.wait()
 
     @pl.loop(0, slots)
     def _(slot):
-        step(CROSS, slot, factor, HEAD)
+        step(CROSS, slot, plan[CROSS][0][0] + HEAD)
 
         @pl.when(slot < lines)
         def _():
@@ -402,7 +396,7 @@
                 columns[index, spot, :] = jnp.broadcast_to(value, (LANES, LANES)).T
 
         for way in (UP, DOWN, KEEP):
-            step(way, slot, factor)
+            step(way, slot)
 
     def t_copy(shift):
         return pltpu.make_async_remote_copy(
@@ -418,13 +412,9 @@
         t_copy(shift).start()
 
     for way in (CROSS, UP, DOWN):
-        @pl.loop(0, sent[way])
+        @pl.loop(0, pick({device: sent[device, way] for device in words}))
         def _(slot):
             copy(way, slot).wait_send()
-
-    @pl.loop(0, chunks)
-    def _(chunk):
-        field_copy(chunk).wait()
 
     for shift in range(1, reals):
         t_copy(shift).wait()
@@ -434,18 +424,13 @@
     mean_out[...] = total / (own_reals * reals)
 
 
-def hand_out_kernel(field_in, mean_in, field_out, mean_out, field, mean, in_sem, out_sem):
-    part = field.shape[1]
-    reads = [pltpu.make_async_copy(mean_in, mean, in_sem.at[PARTS])]
+def hand_out_kernel(field, mean, field_out, mean_out, out_sem):
+    part = field.shape[0] // PARTS
     writes = [pltpu.make_async_copy(mean, mean_out, out_sem.at[PARTS])]
     for index in range(PARTS):
         rows = pl.ds(index * part, part)
-        reads.append(pltpu.make_async_copy(field_in.at[rows, :], field.at[index], in_sem.at[index]))
-        writes.append(pltpu.make_async_copy(field.at[index], field_out.at[rows, :], out_sem.at[index]))
-    for read in reads:
-        read.start()
-    for read, write in zip(reads, writes):
-        read.wait()
+        writes.append(pltpu.make_async_copy(field.at[rows, :], field_out.at[rows, :], out_sem.at[index]))
+    for write in writes:
         write.start()
     for write in writes:
         write.wait()
@@ -455,24 +440,20 @@
     panels, per_column, tile = factor.shape[:3]
     sites, own_reals = epsilon.shape
     count, reals = lax.axis_size("site"), lax.axis_size("real")
-    chunks = sites // ROWS
     lines = sites // LANES
-    words = stream_words(count // PAIR, panels)
-    most = [
-        max(sum(word > 0 for word in own[way][1]) for own in words.values()) * (tile // ROWS // 2)
-        for way in (CROSS, UP, DOWN)
-    ]
+    words, sent = stream_words(count // PAIR, panels, tile // ROWS)
+    most = [max(sent[device, way] for device in words) for way in (CROSS, UP, DOWN)]
     piece = (ROWS, own_reals)
     vmem = pl.BlockSpec(memory_space=pltpu.VMEM)
     anywhere = pl.BlockSpec(memory_space=pl.ANY)
     field, mean = pl.pallas_call(
-        functools.partial(field_kernel, words, own_reals),
+        functools.partial(field_kernel, words, sent, own_reals),
         out_shape=(
-            jax.ShapeDtypeStruct((sites, own_reals), jnp.bfloat16),
-            jax.ShapeDtypeStruct((lines, LANES), jnp.float32),
+            pltpu.VMEM((sites, own_reals), jnp.bfloat16),
+            pltpu.VMEM((lines, LANES), jnp.float32),
         ),
         in_specs=[pl.BlockSpec(memory_space=pltpu.SMEM), anywhere, anywhere, vmem, vmem, vmem],
-        out_specs=(anywhere, vmem),
+        out_specs=(vmem, vmem),
         scratch_shapes=[
             pltpu.VMEM(epsilon.shape, epsilon.dtype),
             pltpu.VMEM(factor.shape, factor.dtype),
@@ -483,12 +464,10 @@
             pltpu.VMEM((3, sites, LANES), jnp.float32),
             pltpu.VMEM((sites, LANES), jnp.float32),
             pltpu.SMEM((2 * panels, SITE_TILES), jnp.int32),
-            pltpu.VMEM((chunks, ROWS, own_reals), jnp.bfloat16),
             pltpu.SemaphoreType.DMA((1 + 2 * panels,)),
             *[pltpu.SemaphoreType.DMA((slots,)) for slots in most + most],
             pltpu.SemaphoreType.DMA((reals,)),
             pltpu.SemaphoreType.DMA((reals,)),
-            pltpu.SemaphoreType.DMA((chunks,)),
         ],
         compiler_params=pltpu.CompilerParams(
             collective_id=0, has_side_effects=True, vmem_limit_bytes=60 * 1024 * 1024
@@ -507,15 +486,10 @@
             jax.ShapeDtypeStruct(field.shape, field.dtype),
             jax.ShapeDtypeStruct(mean.shape, mean.dtype),
         ),
-        in_specs=[anywhere, anywhere],
+        in_specs=[vmem, vmem],
         out_specs=(anywhere, anywhere),
-        scratch_shapes=[
-            pltpu.VMEM((PARTS, sites // PARTS, own_reals), field.dtype),
-            pltpu.VMEM(mean.shape, mean.dtype),
-            pltpu.SemaphoreType.DMA((PARTS + 1,)),
-            pltpu.SemaphoreType.DMA((PARTS + 1,)),
-        ],
-    )(field, mean)
+        scratch_shapes=[pltpu.SemaphoreType.DMA((PARTS + 1,))],
+    )(pltpu.with_memory_space_constraint(field, pltpu.VMEM), pltpu.with_memory_space_constraint(mean, pltpu.VMEM))
     return field, mean.reshape(sites)
 
 

time: 147 us -> 143 us (0.973); the launches traced: 145 us -> 143 us
  Pallas kernels: 144 us -> 142 us
where the time goes in v2:
time: 143 us
  Pallas kernels  142 us (99%)
    pallas_call x1, Pallas kernels, line_shards(): pl.pallas_call(functools.partial(field_kernel, words, sent, own_reals), o...  141 us

profile of v2, /device:TPU:11, one launch (start us, length us, event | category | flops | bytes accessed | tf_op | source)
XLA Modules:
  0.0 142.8 jit_solution(4072121317179846440)
XLA Ops:
  0.6 141.2 %shard_map.77 = (bf16[1024,512]{1,0:T(8,128)(2,1)S(1)}, f32[8,128]{1,0:T(8,128)S(1)}) custom-call(s32[2,9]{1,0:T(2,128)} %block_rows.1, bf16[1024,512]{1,0:T(8,128)(2,1)} %eps_in.1, bf16[2,9,512,512]{3,2,1,0:T(8,128)(2,1)} %factor_in.1, f32[8,128]{1,0:T(8,128)} %bitcast.4, f32[8,128]{1,0:T(8,128)} %bitcast.5, f32[8,128]{1,0:T(8,128)} %bitcast.6), custom_call_target="tpu_custom_call" | custom-call | tf_op jit(solution)/shard_map/pallas_call | solution.py:449
  141.8 1.0 shard_map.78

commit v3 on v2

--- a/solution.py
+++ b/solution.py
@@ -12,6 +12,7 @@
 ROWS = 64
 PARTS = 4
 HEAD = 2
+LEAD = 3
 SITE_TILES = 16
 LAST_OFFSET = 12
 CROSS, UP, DOWN, KEEP = range(4)
@@ -88,52 +89,52 @@
 
 PLAN = {
     (0, 0): (
-        [(0, 22), (4, 23), (10, 12), (14, 13), (18, 6), (23, 20), (27, 4), (35, 21), (42, 15), (49, 5), (54, 7)],
-        [(2, 14), (6, 9), (13, 25), (17, 19), (24, 24), (29, 10), (33, 18), (39, 17), (43, 8), (49, 16), (56, 11)],
+        [(0, 20), (4, 22), (10, 21), (15, 15), (20, 23), (27, 5), (36, 12), (42, 13), (46, 7), (50, 4), (54, 6)],
+        [(4, 25), (8, 10), (15, 18), (20, 19), (27, 24), (35, 14), (38, 11), (43, 8), (47, 17), (51, 16), (55, 9)],
         [],
-        [(31, 2), (44, 3), (48, 0), (56, 1)],
+        [(33, 0), (42, 2), (51, 1), (55, 3)],
     ),
     (0, 1): (
-        [(0, 14), (5, 9), (9, 25), (13, 19), (20, 24), (26, 10), (30, 18), (34, 17), (42, 8), (48, 16), (52, 11)],
-        [(0, 29), (7, 26), (11, 28), (15, 22), (22, 13), (26, 23), (30, 12), (34, 27), (40, 20), (46, 21), (50, 15)],
+        [(0, 25), (4, 10), (8, 18), (12, 19), (20, 24), (28, 14), (31, 11), (35, 8), (39, 17), (43, 16), (47, 9)],
+        [(2, 27), (6, 26), (15, 29), (19, 28), (26, 22), (30, 23), (34, 21), (38, 12), (42, 20), (46, 13), (51, 15)],
         [],
-        [(43, 4), (47, 6), (52, 5), (56, 7)],
+        [(39, 5), (46, 7), (51, 4), (56, 6)],
     ),
     (1, 0): (
-        [(0, 28), (4, 13), (8, 22), (12, 23), (18, 20), (25, 29), (29, 14), (33, 12), (42, 21), (50, 15)],
-        [(1, 30), (5, 31), (10, 25), (14, 19), (18, 26), (24, 24), (28, 18), (39, 17), (44, 27), (51, 16)],
-        [(17, 2), (28, 0), (35, 3), (43, 1)],
-        [(39, 10), (45, 9), (49, 8), (53, 11)],
+        [(3, 28), (7, 22), (11, 20), (17, 23), (23, 12), (30, 29), (35, 21), (45, 14), (48, 13), (52, 15)],
+        [(0, 30), (6, 31), (12, 26), (17, 27), (21, 19), (29, 18), (36, 24), (42, 25), (49, 17), (54, 16)],
+        [(18, 0), (35, 2), (44, 1), (54, 3)],
+        [(37, 11), (44, 8), (48, 10), (56, 9)],
     ),
     (1, 1): (
-        [(1, 17), (5, 2), (9, 25), (13, 24), (18, 26), (24, 0), (31, 3), (35, 1), (43, 27), (47, 16)],
-        [(0, 31), (5, 19), (10, 28), (16, 22), (22, 30), (28, 18), (35, 29), (41, 23), (45, 20), (55, 21)],
-        [(25, 4), (31, 6), (45, 5), (54, 7)],
-        [(35, 13), (39, 14), (51, 12), (56, 15)],
+        [(2, 24), (8, 27), (12, 26), (16, 0), (20, 25), (24, 2), (28, 16), (32, 1), (39, 17), (48, 3)],
+        [(1, 30), (5, 19), (13, 18), (18, 31), (25, 28), (32, 23), (36, 29), (40, 22), (46, 20), (53, 21)],
+        [(30, 5), (35, 7), (42, 6), (50, 4)],
+        [(42, 12), (47, 14), (50, 13), (54, 15)],
     ),
     (2, 0): (
-        [(0, 6), (4, 4), (8, 22), (12, 28), (21, 5), (25, 7), (37, 29), (43, 23), (47, 21), (51, 20)],
-        [(10, 31), (14, 25), (26, 26), (33, 30), (37, 24), (53, 27)],
-        [(5, 0), (10, 2), (15, 14), (23, 1), (27, 3), (38, 10), (42, 9), (46, 8), (53, 11)],
+        [(0, 7), (4, 28), (9, 6), (13, 22), (18, 5), (24, 23), (29, 29), (36, 4), (46, 20), (52, 21)],
+        [(10, 31), (14, 30), (22, 27), (37, 26), (48, 25), (54, 24)],
+        [(8, 0), (12, 11), (18, 14), (21, 1), (27, 2), (37, 8), (43, 10), (50, 3), (54, 9)],
         [(47, 19), (51, 18), (55, 17), (59, 16)],
     ),
     (2, 1): (
-        [(0, 26), (4, 24), (9, 25), (14, 9), (20, 10), (25, 8), (34, 27), (38, 19), (42, 11), (47, 18)],
-        [(16, 31), (37, 28), (43, 29), (47, 30)],
-        [(0, 0), (4, 2), (8, 1), (12, 3), (22, 6), (26, 4), (31, 13), (37, 12), (42, 5), (47, 7), (51, 15)],
-        [(43, 22), (47, 23), (52, 20), (56, 21)],
+        [(0, 27), (4, 11), (8, 25), (12, 8), (19, 10), (28, 24), (34, 26), (40, 19), (49, 18), (53, 9)],
+        [(5, 30), (32, 28), (36, 31), (44, 29)],
+        [(0, 1), (4, 2), (8, 0), (13, 6), (20, 3), (29, 5), (33, 7), (38, 12), (42, 13), (48, 4), (52, 15)],
+        [(40, 23), (48, 22), (52, 20), (56, 21)],
     ),
     (3, 0): (
-        [(0, 5), (4, 6), (9, 4), (13, 13), (17, 12), (24, 28), (29, 31), (35, 7), (40, 15), (47, 30), (53, 29)],
+        [(0, 5), (4, 6), (8, 12), (14, 31), (21, 7), (27, 13), (31, 15), (38, 4), (42, 28), (46, 29), (52, 30)],
         [],
-        [(3, 2), (7, 0), (12, 14), (16, 11), (22, 1), (27, 3), (34, 10), (40, 9), (46, 8), (50, 16), (54, 17)],
-        [(40, 26), (46, 24), (50, 25), (56, 27)],
+        [(2, 0), (6, 11), (13, 1), (21, 14), (26, 2), (32, 10), (37, 8), (41, 9), (45, 3), (49, 17), (53, 16)],
+        [(43, 26), (47, 27), (51, 25), (55, 24)],
     ),
     (3, 1): (
-        [(0, 2), (4, 0), (8, 14), (13, 11), (19, 1), (23, 3), (27, 10), (32, 9), (36, 8), (44, 16), (50, 17)],
+        [(0, 0), (4, 11), (10, 1), (14, 14), (17, 2), (21, 10), (27, 8), (31, 9), (38, 3), (44, 17), (48, 16)],
         [],
-        [(0, 19), (4, 5), (8, 18), (20, 6), (24, 4), (29, 13), (33, 12), (39, 20), (43, 7), (47, 15), (54, 21)],
-        [(39, 31), (44, 28), (51, 30), (55, 29)],
+        [(0, 18), (4, 19), (8, 6), (12, 20), (22, 5), (26, 7), (30, 12), (34, 13), (39, 4), (44, 15), (54, 21)],
+        [(37, 31), (44, 28), (52, 29), (56, 30)],
     ),
 }
 
@@ -188,7 +189,7 @@
                 bases[target(device, way), unit, way] = base
                 base += pieces(unit, per_tile)[1]
             sent[device, way] = base
-    words = {}
+    words, leads = {}, {}
     for device, streams in PLAN.items():
         planned = [unit for stream in streams for _, unit in stream]
         assert sorted(planned) == sorted(steps[device])
@@ -206,15 +207,18 @@
                 two = sum((1 + 2 * bases[device, unit, kind]) * 128**kind for kind in arriving)
                 line.append((start, length, one, two))
             words[device].append(line)
-        own, arriving, _ = steps[device][streams[CROSS][0][1]]
-        assert own and not arriving
-    return words, sent
+        for way in (CROSS, UP, DOWN):
+            start, unit = (streams[way] or [(2**20, 0)])[0]
+            own, arriving, _ = steps[device].get(unit, (False, (), way))
+            leads[device, way] = own and not arriving and start <= LEAD
+            assert not leads[device, way] or pieces(unit, per_tile)[0] == pieces(streams[CROSS][0][1], per_tile)[0]
+    return words, sent, leads
 
 
 def field_kernel(
-    words, sent, own_reals, block_rows, eps_in, factor_in, median, spread, critical, field, mean_out,
-    eps, factor, head, x_out, u_out, d_out, x_in, u_in, d_in, spare, totals, columns, folds, table,
-    load_sem, x_send, u_send, d_send, x_recv, u_recv, d_recv, t_send, t_recv,
+    words, sent, leads, own_reals, rows_in, eps_in, factor_in, median_in, spread_in, critical_in, field, mean_out,
+    block_rows, sites_in, eps, factor, head, x_out, u_out, d_out, x_in, u_in, d_in, spare, totals, columns, folds, table,
+    load_sem, site_sem, x_send, u_send, d_send, x_recv, u_recv, d_recv, t_send, t_recv,
 ):
     panels, per_column, tile = factor.shape[0], factor.shape[1], factor.shape[2]
     depth = len(words) // PAIR
@@ -234,6 +238,19 @@
             result = value if result is None else jnp.where(here[device], value, result)
         return result
 
+    barrier = pltpu.get_barrier_semaphore()
+    pl.semaphore_signal(barrier, inc=1, device_id={"site": site + 1 - 2 * x}, device_id_type=MESH)
+    for shift in range(1, reals):
+        pl.semaphore_signal(barrier, inc=1, device_id={"real": (me + shift) % reals}, device_id_type=MESH)
+
+    @pl.when(z > 0)
+    def _():
+        pl.semaphore_signal(barrier, inc=1, device_id={"site": site - PAIR}, device_id_type=MESH)
+
+    @pl.when(z < depth - 1)
+    def _():
+        pl.semaphore_signal(barrier, inc=1, device_id={"site": site + PAIR}, device_id_type=MESH)
+
     begin = pick({device: own[CROSS][0][2] // 16 % 8 * ROWS for device, own in words.items()})
     first = [pltpu.make_async_copy(eps_in, eps, load_sem.at[0])]
     rest = []
@@ -245,21 +262,11 @@
         rest.append(pltpu.make_async_copy(
             factor_in.at[panel], factor.at[panel], load_sem.at[1 + panels + panel]
         ))
-    for load in first + rest:
+    known = [pltpu.make_async_copy(rows_in, block_rows, site_sem.at[0])]
+    for index, ref in enumerate((median_in, spread_in, critical_in)):
+        known.append(pltpu.make_async_copy(ref, sites_in.at[index], site_sem.at[1 + index]))
+    for load in known + first + rest:
         load.start()
-
-    barrier = pltpu.get_barrier_semaphore()
-    pl.semaphore_signal(barrier, inc=1, device_id={"site": site + 1 - 2 * x}, device_id_type=MESH)
-    for shift in range(1, reals):
-        pl.semaphore_signal(barrier, inc=1, device_id={"real": (me + shift) % reals}, device_id_type=MESH)
-
-    @pl.when(z > 0)
-    def _():
-        pl.semaphore_signal(barrier, inc=1, device_id={"site": site - PAIR}, device_id_type=MESH)
-
-    @pl.when(z < depth - 1)
-    def _():
-        pl.semaphore_signal(barrier, inc=1, device_id={"site": site + PAIR}, device_id_type=MESH)
 
     plan, slots = [], 0
     for way in range(4):
@@ -271,6 +278,8 @@
         ])
         slots = max([slots] + [own[way][-1][0] + own[way][-1][1] for own in words.values() if own[way]])
 
+    for load in known:
+        load.wait()
     for panel in range(panels):
         begins = [
             (block_rows[panel, block] - site * panels + panels * count) % (panels * count)
@@ -375,28 +384,39 @@
 
     for load in first:
         load.wait()
+    ahead = [pick({device: leads[device, way] for device in words}) for way in (CROSS, UP, DOWN)]
     for turn in range(HEAD):
-        multiply(x_out.at[turn], bits(plan[CROSS][0][2], 0, 4), turn, head)
-    pl.semaphore_wait(barrier, reals + jnp.where(z > 0, 1, 0) + jnp.where(z < depth - 1, 1, 0))
-    for turn in range(HEAD):
-        copy(CROSS, turn).start()
+        for way in (CROSS, UP, DOWN):
+            @pl.when(ahead[way] == 1)
+            def _():
+                multiply(ways[way][0].at[turn], bits(plan[way][0][2], 0, 4), turn, head)
+
+        if turn == 0:
+            pl.semaphore_wait(barrier, reals + jnp.where(z > 0, 1, 0) + jnp.where(z < depth - 1, 1, 0))
+
+        for way in (CROSS, UP, DOWN):
+            @pl.when(ahead[way] == 1)
+            def _():
+                copy(way, turn).start()
+
     for load in rest:
         load.wait()
 
     @pl.loop(0, slots)
     def _(slot):
-        step(CROSS, slot, plan[CROSS][0][0] + HEAD)
+        step(CROSS, slot, plan[CROSS][0][0] + HEAD * ahead[CROSS])
 
         @pl.when(slot < lines)
         def _():
             spot = pl.ds(pl.multiple_of(slot * LANES, LANES), LANES)
-            for index, ref in enumerate((median, spread, critical)):
-                value = ref[pl.ds(slot, 1), :]
+            for index in range(3):
+                value = sites_in[index, pl.ds(slot, 1), :]
                 value = jnp.log(value) if index == 2 else value
                 columns[index, spot, :] = jnp.broadcast_to(value, (LANES, LANES)).T
 
-        for way in (UP, DOWN, KEEP):
-            step(way, slot)
+        for way in (UP, DOWN):
+            step(way, slot, plan[way][0][0] + HEAD * ahead[way])
+        step(KEEP, slot)
 
     def t_copy(shift):
         return pltpu.make_async_remote_copy(
@@ -441,20 +461,22 @@
     sites, own_reals = epsilon.shape
     count, reals = lax.axis_size("site"), lax.axis_size("real")
     lines = sites // LANES
-    words, sent = stream_words(count // PAIR, panels, tile // ROWS)
+    words, sent, leads = stream_words(count // PAIR, panels, tile // ROWS)
     most = [max(sent[device, way] for device in words) for way in (CROSS, UP, DOWN)]
     piece = (ROWS, own_reals)
     vmem = pl.BlockSpec(memory_space=pltpu.VMEM)
     anywhere = pl.BlockSpec(memory_space=pl.ANY)
     field, mean = pl.pallas_call(
-        functools.partial(field_kernel, words, sent, own_reals),
+        functools.partial(field_kernel, words, sent, leads, own_reals),
         out_shape=(
             pltpu.VMEM((sites, own_reals), jnp.bfloat16),
             pltpu.VMEM((lines, LANES), jnp.float32),
         ),
-        in_specs=[pl.BlockSpec(memory_space=pltpu.SMEM), anywhere, anywhere, vmem, vmem, vmem],
+        in_specs=[anywhere] * 6,
         out_specs=(vmem, vmem),
         scratch_shapes=[
+            pltpu.SMEM(block_rows.shape, block_rows.dtype),
+            pltpu.VMEM((3, lines, LANES), jnp.float32),
             pltpu.VMEM(epsilon.shape, epsilon.dtype),
             pltpu.VMEM(factor.shape, factor.dtype),
             pltpu.VMEM((panels, per_column, HEAD * ROWS, tile), factor.dtype),
@@ -465,6 +487,7 @@
             pltpu.VMEM((sites, LANES), jnp.float32),
             pltpu.SMEM((2 * panels, SITE_TILES), jnp.int32),
             pltpu.SemaphoreType.DMA((1 + 2 * panels,)),
+            pltpu.SemaphoreType.DMA((4,)),
             *[pltpu.SemaphoreType.DMA((slots,)) for slots in most + most],
             pltpu.SemaphoreType.DMA((reals,)),
             pltpu.SemaphoreType.DMA((reals,)),

time: 143 us -> 141 us (0.986)
  Pallas kernels: 142 us -> 140 us
    pallas_call x1, Pallas kernels: 141 us -> 139 us  [line_shards(): pl.pallas_call(functools.partial(field_kernel, words, sent, leads, own_re...]
where the time goes in v3:
time: 141 us
  Pallas kernels  140 us (99%)
    pallas_call x1, Pallas kernels, line_shards(): pl.pallas_call(functools.partial(field_kernel, words, sent, leads, own_re...  139 us

profile of v3, /device:TPU:11, one launch (start us, length us, event | category | flops | bytes accessed | tf_op | source)
XLA Modules:
  0.0 141.1 jit_solution(9502005955471096694)
XLA Ops:
  0.6 139.4 %shard_map.77 = (bf16[1024,512]{1,0:T(8,128)(2,1)S(1)}, f32[8,128]{1,0:T(8,128)S(1)}) custom-call(s32[2,9]{1,0:T(2,128)} %rows_in.1, bf16[1024,512]{1,0:T(8,128)(2,1)} %eps_in.1, bf16[2,9,512,512]{3,2,1,0:T(8,128)(2,1)} %factor_in.1, f32[8,128]{1,0:T(8,128)} %bitcast.4, f32[8,128]{1,0:T(8,128)} %bitcast.5, f32[8,128]{1,0:T(8,128)} %bitcast.6), custom_call_target="tpu_custom_call" | custom-call | tf_op jit(solution)/shard_map/pallas_call | solution.py:469
  140.0 1.0 shard_map.78

commit v4 on v3

--- a/solution.py
+++ b/solution.py
@@ -303,13 +303,12 @@
         @pl.when(relative <= LAST_OFFSET)
         def _():
             row = pl.multiple_of(piece * ROWS, ROWS)
-            result = None
-            for panel in range(panels):
-                block = source[panel, table[panel, relative], pl.ds(row, ROWS), :]
-                product = jnp.dot(
-                    block, eps[panel * tile:(panel + 1) * tile, :], preferred_element_type=jnp.float32
-                ) * table[panels + panel, relative].astype(jnp.float32)
-                result = product if result is None else result + product
+            blocks = [
+                source[panel, table[panel, relative], pl.ds(row, ROWS), :]
+                * table[panels + panel, relative].astype(jnp.float32).astype(source.dtype)
+                for panel in range(panels)
+            ]
+            result = jnp.dot(jnp.concatenate(blocks, axis=1), eps[...], preferred_element_type=jnp.float32)
             out[...] = result
 
         @pl.when(relative > LAST_OFFSET)

time: 141 us -> 141 us (level)
  no operation moved by 1% of the time
where the time goes in v4:
time: 141 us
  Pallas kernels  140 us (99%)
    pallas_call x1, Pallas kernels, line_shards(): pl.pallas_call(functools.partial(field_kernel, words, sent, leads, own_re...  139 us

profile of v4, /device:TPU:11, one launch (start us, length us, event | category | flops | bytes accessed | tf_op | source)
XLA Modules:
  0.0 141.0 jit_solution(1330980218251055700)
XLA Ops:
  0.6 139.4 %shard_map.77 = (bf16[1024,512]{1,0:T(8,128)(2,1)S(1)}, f32[8,128]{1,0:T(8,128)S(1)}) custom-call(s32[2,9]{1,0:T(2,128)} %rows_in.1, bf16[1024,512]{1,0:T(8,128)(2,1)} %eps_in.1, bf16[2,9,512,512]{3,2,1,0:T(8,128)(2,1)} %factor_in.1, f32[8,128]{1,0:T(8,128)} %bitcast.4, f32[8,128]{1,0:T(8,128)} %bitcast.5, f32[8,128]{1,0:T(8,128)} %bitcast.6), custom_call_target="tpu_custom_call" | custom-call | tf_op jit(solution)/shard_map/pallas_call | solution.py:468
  140.0 1.0 shard_map.78

commit v5 on v4

--- a/solution.py
+++ b/solution.py
@@ -89,52 +89,52 @@
 
 PLAN = {
     (0, 0): (
-        [(0, 20), (4, 22), (10, 21), (15, 15), (20, 23), (27, 5), (36, 12), (42, 13), (46, 7), (50, 4), (54, 6)],
-        [(4, 25), (8, 10), (15, 18), (20, 19), (27, 24), (35, 14), (38, 11), (43, 8), (47, 17), (51, 16), (55, 9)],
+        [(0, 20, 0), (4, 22, 0), (10, 21, 0), (15, 15, 0), (20, 23, 0), (27, 5, 0), (36, 12, 0), (42, 13, 0), (46, 7, 0), (50, 4, 0), (54, 6, 0)],
+        [(4, 25, 0), (8, 10, 0), (15, 18, 0), (20, 19, 0), (27, 24, 0), (35, 14, 0), (38, 11, 0), (43, 8, 0), (47, 17, 0), (51, 16, 0), (55, 9, 0)],
         [],
-        [(33, 0), (42, 2), (51, 1), (55, 3)],
+        [(33, 0, 0), (42, 2, 0), (51, 1, 0), (55, 3, 0)],
     ),
     (0, 1): (
-        [(0, 25), (4, 10), (8, 18), (12, 19), (20, 24), (28, 14), (31, 11), (35, 8), (39, 17), (43, 16), (47, 9)],
-        [(2, 27), (6, 26), (15, 29), (19, 28), (26, 22), (30, 23), (34, 21), (38, 12), (42, 20), (46, 13), (51, 15)],
+        [(0, 25, 0), (4, 10, 0), (8, 18, 0), (12, 19, 0), (20, 24, 0), (28, 14, 0), (31, 11, 0), (35, 8, 0), (39, 17, 0), (43, 16, 0), (47, 9, 0)],
+        [(2, 27, 0), (6, 26, 1), (15, 29, 1), (19, 28, 1), (26, 22, 1), (30, 23, 1), (34, 21, 1), (38, 12, 0), (42, 20, 0), (46, 13, 0), (51, 15, 0)],
         [],
-        [(39, 5), (46, 7), (51, 4), (56, 6)],
+        [(39, 5, 0), (46, 7, 0), (51, 4, 0), (56, 6, 0)],
     ),
     (1, 0): (
-        [(3, 28), (7, 22), (11, 20), (17, 23), (23, 12), (30, 29), (35, 21), (45, 14), (48, 13), (52, 15)],
-        [(0, 30), (6, 31), (12, 26), (17, 27), (21, 19), (29, 18), (36, 24), (42, 25), (49, 17), (54, 16)],
-        [(18, 0), (35, 2), (44, 1), (54, 3)],
-        [(37, 11), (44, 8), (48, 10), (56, 9)],
+        [(3, 28, 0), (7, 22, 0), (11, 20, 0), (17, 23, 0), (23, 12, 0), (30, 29, 0), (35, 21, 0), (45, 14, 0), (48, 13, 0), (52, 15, 0)],
+        [(0, 30, 0), (6, 31, 0), (12, 26, 0), (17, 27, 0), (21, 19, 0), (29, 18, 0), (36, 24, 0), (42, 25, 0), (49, 17, 0), (54, 16, 0)],
+        [(18, 0, 0), (35, 2, 0), (44, 1, 0), (54, 3, 0)],
+        [(37, 11, 0), (44, 8, 0), (48, 10, 0), (56, 9, 0)],
     ),
     (1, 1): (
-        [(2, 24), (8, 27), (12, 26), (16, 0), (20, 25), (24, 2), (28, 16), (32, 1), (39, 17), (48, 3)],
-        [(1, 30), (5, 19), (13, 18), (18, 31), (25, 28), (32, 23), (36, 29), (40, 22), (46, 20), (53, 21)],
-        [(30, 5), (35, 7), (42, 6), (50, 4)],
-        [(42, 12), (47, 14), (50, 13), (54, 15)],
+        [(2, 24, 0), (8, 27, 0), (12, 26, 0), (16, 0, 0), (20, 25, 0), (24, 2, 0), (28, 16, 0), (32, 1, 0), (39, 17, 0), (48, 3, 0)],
+        [(1, 30, 0), (5, 19, 0), (13, 18, 0), (18, 31, 0), (25, 28, 0), (32, 23, 0), (36, 29, 0), (40, 22, 0), (46, 20, 0), (53, 21, 0)],
+        [(30, 5, 0), (35, 7, 0), (42, 6, 0), (50, 4, 0)],
+        [(42, 12, 0), (47, 14, 0), (50, 13, 0), (54, 15, 0)],
     ),
     (2, 0): (
-        [(0, 7), (4, 28), (9, 6), (13, 22), (18, 5), (24, 23), (29, 29), (36, 4), (46, 20), (52, 21)],
-        [(10, 31), (14, 30), (22, 27), (37, 26), (48, 25), (54, 24)],
-        [(8, 0), (12, 11), (18, 14), (21, 1), (27, 2), (37, 8), (43, 10), (50, 3), (54, 9)],
-        [(47, 19), (51, 18), (55, 17), (59, 16)],
+        [(0, 7, 0), (4, 28, 0), (9, 6, 0), (13, 22, 0), (18, 5, 0), (24, 23, 0), (29, 29, 0), (36, 4, 0), (46, 20, 0), (52, 21, 0)],
+        [(10, 31, 0), (14, 30, 0), (22, 27, 0), (37, 26, 0), (48, 25, 0), (54, 24, 0)],
+        [(8, 0, 0), (12, 11, 0), (18, 14, 0), (21, 1, 0), (27, 2, 0), (37, 8, 0), (43, 10, 0), (50, 3, 0), (54, 9, 0)],
+        [(47, 19, 0), (51, 18, 0), (55, 17, 0), (59, 16, 0)],
     ),
     (2, 1): (
-        [(0, 27), (4, 11), (8, 25), (12, 8), (19, 10), (28, 24), (34, 26), (40, 19), (49, 18), (53, 9)],
-        [(5, 30), (32, 28), (36, 31), (44, 29)],
-        [(0, 1), (4, 2), (8, 0), (13, 6), (20, 3), (29, 5), (33, 7), (38, 12), (42, 13), (48, 4), (52, 15)],
-        [(40, 23), (48, 22), (52, 20), (56, 21)],
+        [(0, 27, 0), (4, 11, 0), (8, 25, 0), (12, 8, 0), (19, 10, 0), (28, 24, 0), (34, 26, 0), (40, 19, 0), (49, 18, 0), (53, 9, 0)],
+        [(5, 30, 0), (32, 28, 0), (36, 31, 0), (44, 29, 0)],
+        [(0, 1, 0), (4, 2, 0), (8, 0, 0), (13, 6, 0), (20, 3, 0), (29, 5, 0), (33, 7, 0), (38, 12, 0), (42, 13, 0), (48, 4, 0), (52, 15, 0)],
+        [(40, 23, 0), (48, 22, 0), (52, 20, 0), (56, 21, 0)],
     ),
     (3, 0): (
-        [(0, 5), (4, 6), (8, 12), (14, 31), (21, 7), (27, 13), (31, 15), (38, 4), (42, 28), (46, 29), (52, 30)],
+        [(0, 5, 0), (4, 6, 0), (8, 12, 0), (14, 31, 0), (21, 7, 0), (27, 13, 0), (31, 15, 0), (38, 4, 0), (42, 28, 0), (46, 29, 0), (52, 30, 0)],
         [],
-        [(2, 0), (6, 11), (13, 1), (21, 14), (26, 2), (32, 10), (37, 8), (41, 9), (45, 3), (49, 17), (53, 16)],
-        [(43, 26), (47, 27), (51, 25), (55, 24)],
+        [(2, 0, 0), (6, 11, 0), (13, 1, 0), (21, 14, 0), (26, 2, 0), (32, 10, 0), (37, 8, 0), (41, 9, 0), (45, 3, 0), (49, 17, 0), (53, 16, 0)],
+        [(43, 26, 0), (47, 27, 0), (51, 25, 0), (55, 24, 0)],
     ),
     (3, 1): (
-        [(0, 0), (4, 11), (10, 1), (14, 14), (17, 2), (21, 10), (27, 8), (31, 9), (38, 3), (44, 17), (48, 16)],
+        [(0, 0, 0), (4, 11, 0), (10, 1, 0), (14, 14, 0), (17, 2, 0), (21, 10, 0), (27, 8, 0), (31, 9, 0), (38, 3, 0), (44, 17, 0), (48, 16, 0)],
         [],
-        [(0, 18), (4, 19), (8, 6), (12, 20), (22, 5), (26, 7), (30, 12), (34, 13), (39, 4), (44, 15), (54, 21)],
-        [(37, 31), (44, 28), (52, 29), (56, 30)],
+        [(0, 18, 0), (4, 19, 1), (8, 6, 1), (12, 20, 1), (22, 5, 1), (26, 7, 1), (30, 12, 1), (34, 13, 1), (39, 4, 0), (44, 15, 0), (54, 21, 0)],
+        [(37, 31, 0), (44, 28, 0), (52, 29, 0), (56, 30, 0)],
     ),
 }
 
@@ -180,35 +180,39 @@
         z, x = device
         return {CROSS: (z, 1 - x), UP: (z + 1, x), DOWN: (z - 1, x)}[way]
 
-    bases, sent = {}, {}
+    bases, paired, sent = {}, {}, {}
     for device, streams in PLAN.items():
         for way in (CROSS, UP, DOWN):
             base = 0
-            for _, unit in streams[way]:
+            for number, (_, unit, pairs) in enumerate(streams[way]):
                 assert steps[device][unit][2] == way
+                assert not pairs or (number and pieces(unit, per_tile)[1] % 2 == 0)
+                paired[target(device, way), unit, way] = pairs
                 bases[target(device, way), unit, way] = base
                 base += pieces(unit, per_tile)[1]
             sent[device, way] = base
     words, leads = {}, {}
     for device, streams in PLAN.items():
-        planned = [unit for stream in streams for _, unit in stream]
+        planned = [unit for stream in streams for _, unit, _ in stream]
         assert sorted(planned) == sorted(steps[device])
         origin, words[device] = panels * (PAIR * device[0] + device[1]), []
         for way, stream in enumerate(streams):
             line, free = [], 0
-            for start, unit in stream:
+            for start, unit, pairs in stream:
                 own, arriving, onward = steps[device][unit]
                 begin, length = pieces(unit, per_tile)
                 start = start * per_tile // 8
                 assert onward == way and start >= free
                 free = start + length
                 base = 0 if way == KEEP else bases[target(device, way), unit, way]
-                one = (unit // 2 - origin) % SITE_TILES + 16 * begin + 128 * base
-                two = sum((1 + 2 * bases[device, unit, kind]) * 128**kind for kind in arriving)
+                one = (unit // 2 - origin) % SITE_TILES + 16 * begin + 128 * base + 8192 * pairs
+                two = sum(
+                    (1 + 2 * bases[device, unit, kind] + 128 * paired[device, unit, kind]) * 256**kind for kind in arriving
+                )
                 line.append((start, length, one, two))
             words[device].append(line)
         for way in (CROSS, UP, DOWN):
-            start, unit = (streams[way] or [(2**20, 0)])[0]
+            start, unit, _ = (streams[way] or [(2**20, 0, 0)])[0]
             own, arriving, _ = steps[device].get(unit, (False, (), way))
             leads[device, way] = own and not arriving and start <= LEAD
             assert not leads[device, way] or pieces(unit, per_tile)[0] == pieces(streams[CROSS][0][1], per_tile)[0]
@@ -321,11 +325,11 @@
         (d_out, d_in, d_send, d_recv, (site + count - PAIR) % count),
     )
 
-    def copy(way, slot):
+    def copy(way, slot, extent=1):
         leaving, landing, departure, arrival, there = ways[way]
         return pltpu.make_async_remote_copy(
-            src_ref=leaving.at[slot],
-            dst_ref=landing.at[slot],
+            src_ref=leaving.at[pl.ds(slot, extent)],
+            dst_ref=landing.at[pl.ds(slot, extent)],
             send_sem=departure.at[slot],
             recv_sem=arrival.at[slot],
             device_id={"site": there},
@@ -370,16 +374,32 @@
             out = spare if way == KEEP else ways[way][0].at[place]
             multiply(out, relative, piece, factor)
             for kind in range(3):
-                @pl.when(bits(two, 7 * kind, 1) == 1)
+                @pl.when(bits(two, 8 * kind, 1) == 1)
                 def _():
-                    arrived = bits(two, 7 * kind + 1, 6) + turn
-                    copy(kind, arrived).wait_recv()
+                    arrived = bits(two, 8 * kind + 1, 6) + turn
+                    of_pair = bits(two, 8 * kind + 7, 1)
+
+                    @pl.when(of_pair == 0)
+                    def _():
+                        copy(kind, arrived).wait_recv()
+
+                    @pl.when(jnp.logical_and(of_pair == 1, turn % 2 == 0))
+                    def _():
+                        copy(kind, arrived, 2).wait_recv()
+
                     out[...] = out[...] + ways[kind][1][arrived]
 
             if way == KEEP:
                 keep(relative * per_tile + piece)
-            else:
+                return
+
+            @pl.when(bits(one, 13, 1) == 0)
+            def _():
                 copy(way, place).start()
+
+            @pl.when(jnp.logical_and(bits(one, 13, 1) == 1, turn % 2 == 1))
+            def _():
+                copy(way, place - 1, 2).start()
 
     for load in first:
         load.wait()
@@ -431,9 +451,18 @@
         t_copy(shift).start()
 
     for way in (CROSS, UP, DOWN):
-        @pl.loop(0, pick({device: sent[device, way] for device in words}))
-        def _(slot):
-            copy(way, slot).wait_send()
+        for _, length, one, _ in plan[way]:
+            @pl.loop(0, length)
+            def _(turn):
+                place = bits(one, 7, 6) + turn
+
+                @pl.when(bits(one, 13, 1) == 0)
+                def _():
+                    copy(way, place).wait_send()
+
+                @pl.when(jnp.logical_and(bits(one, 13, 1) == 1, turn % 2 == 0))
+                def _():
+                    copy(way, place, 2).wait_send()
 
     for shift in range(1, reals):
         t_copy(shift).wait()

time: 141 us -> 141 us (level)
  no operation moved by 1% of the time
where the time goes in v5:
time: 141 us
  Pallas kernels  140 us (99%)
    pallas_call x1, Pallas kernels, line_shards(): pl.pallas_call(functools.partial(field_kernel, words, sent, leads, own_re...  139 us

profile of v5, /device:TPU:11, one launch (start us, length us, event | category | flops | bytes accessed | tf_op | source)
XLA Modules:
  0.0 141.0 jit_solution(12501406712686055263)
XLA Ops:
  0.6 139.4 %shard_map.77 = (bf16[1024,512]{1,0:T(8,128)(2,1)S(1)}, f32[8,128]{1,0:T(8,128)S(1)}) custom-call(s32[2,9]{1,0:T(2,128)} %rows_in.1, bf16[1024,512]{1,0:T(8,128)(2,1)} %eps_in.1, bf16[2,9,512,512]{3,2,1,0:T(8,128)(2,1)} %factor_in.1, f32[8,128]{1,0:T(8,128)} %bitcast.4, f32[8,128]{1,0:T(8,128)} %bitcast.5, f32[8,128]{1,0:T(8,128)} %bitcast.6), custom_call_target="tpu_custom_call" | custom-call | tf_op jit(solution)/shard_map/pallas_call | solution.py:497
  140.0 1.0 shard_map.78
